TPU v7x, 32 devices: a whole 2x2x4 slice. The times are simulated.
32 devices in a mesh: group: 2 (over core), expert: 8 (over z, y), dp: 2 (over x).
Axes of the slice: x: 2, y: 2, z: 4, core: 2. Of those that a mesh axis runs over, the one named last changes fastest.
Arguments:
- tokens: bfloat16 [512, 5120], P(('group', 'expert'), 'dp'), may hold values from -6 to 6
- grad_out: bfloat16 [512, 5120], P(('group', 'expert'), 'dp'), may hold values from -6 to 6
- expert_ids: int32 [512, 8], replicated, may hold values from 0 to 15, as said below
- gate_score: float32 [512, 8], replicated, may hold values from -6 to 6
- w_gate_up: bfloat16 [16, 5120, 2, 1024], P(('group', 'expert'), 'dp'), may hold values from -0.078125 to 0.078125
- w_down: bfloat16 [16, 1024, 5120], P(('group', 'expert'), None, 'dp'), may hold values from -0.1875 to 0.1875
Outputs:
- layer_out: bfloat16 [512, 5120], P(('group', 'expert'), 'dp')
- grad_in: bfloat16 [512, 5120], P(('group', 'expert'), 'dp')
Inputs may be any that keep to these rules, and one draw needn't show every extreme that they name: `expert_ids`: each row names 8 distinct experts, expert number = group * 8 + index, lying in exactly 1 group with 8 experts in each, listed by rising group. In every aligned block of 32 rows each group is named by exactly half of the rows. For a group g and an index e, among the rows of the blocks numbered j * 8 + e (j from 0 to 1) that name group g, no expert of g is named more than 32 times, and some expert of g exactly 32 times.
All inputs are finite; a program needn't handle non-finite values.
Results may differ from a plain program's by a relative error of at most 0.0057.
Values may be sent and summed in bfloat16 or wider, within the bound.
A program may use at most 64 MiB of HBM per device.

v0:
```python
import functools

import jax
import jax.numpy as jnp
from jax import lax
from jax.experimental import pallas as pl
from jax.experimental.pallas import tpu as pltpu
from jax.sharding import PartitionSpec as P

HIGHEST = lax.Precision.HIGHEST


def route_weights(gate_score):
    sigmoid_score = jax.nn.sigmoid(gate_score)
    return 2.5 * sigmoid_score / jnp.sum(sigmoid_score, axis=1, keepdims=True)


def slot_matrix(marked, places):
    running = jnp.cumsum(marked.astype(jnp.int32), axis=-2) - 1
    slot_range = jnp.arange(places, dtype=jnp.int32)
    matched = marked[..., None] & (running[..., None] == slot_range)
    return jnp.moveaxis(matched, -3, -1).astype(jnp.float32)


def local_grad(gate_pre, up_pre, hidden_grad):
    sigmoid_gate = jax.nn.sigmoid(gate_pre)
    gate_grad = hidden_grad * up_pre * sigmoid_gate * (1.0 + gate_pre * (1.0 - sigmoid_gate))
    up_grad = hidden_grad * gate_pre * sigmoid_gate
    return jnp.stack([gate_grad, up_grad], axis=1).astype(jnp.bfloat16)


def across(blocks):
    return lax.all_to_all(blocks, "group", split_axis=0, concat_axis=0, tiled=True)


def within(blocks):
    return lax.all_to_all(blocks, "expert", split_axis=0, concat_axis=0, tiled=True)


def share_sum(partial_value):
    return lax.psum_scatter(partial_value, "dp", scatter_dimension=2, tiled=True)


def share_fold(shares, step_fn, start_value):
    return step_fn(start_value, lax.all_gather(shares, "dp", axis=2, tiled=True), jnp.int32(0))


MESH = pl.DeviceIdType.MESH
LANES = 2
CUTS = 2


def greet(groups, me, lines):
    my_group = lax.axis_index("group")
    line = me // LANES
    barrier = pltpu.get_barrier_semaphore()

    def hello(where):
        pl.semaphore_signal(barrier, inc=1, device_id=where, device_id_type=MESH)

    for step in range(1, groups):
        hello({"group": lax.rem(my_group + step, groups)})
    hello({"expert": line * LANES + 1 - lax.rem(me, LANES)})

    @pl.when(line < lines - 1)
    def _():
        hello({"expert": me + LANES})

    @pl.when(line > 0)
    def _():
        hello({"expert": me - LANES})

    ends = (line < lines - 1).astype(jnp.int32) + (line > 0).astype(jnp.int32)
    pl.semaphore_wait(barrier, groups + ends)


def gather_kernel(groups, members, leaving, out, own_sem, pair_send, pair_recv, send, recv):
    lines = members // LANES
    my_group = lax.axis_index("group")
    me = lax.axis_index("expert")
    line, lane = me // LANES, lax.rem(me, LANES)
    beside = line * LANES + 1 - lane
    greet(groups, me, lines)

    def pair_copy(step, cut):
        other = lax.rem(my_group + step, groups)
        return pltpu.make_async_remote_copy(
            src_ref=leaving.at[other * CUTS + cut],
            dst_ref=out.at[me, my_group * CUTS + cut],
            send_sem=pair_send.at[step, cut],
            recv_sem=pair_recv.at[step, cut],
            device_id={"group": other},
            device_id_type=MESH,
        )

    def pair_wait(step, cut):
        source = lax.rem(my_group + groups - step, groups)
        pltpu.make_async_remote_copy(
            src_ref=leaving.at[source * CUTS + cut],
            dst_ref=out.at[me, source * CUTS + cut],
            send_sem=pair_send.at[step, cut],
            recv_sem=pair_recv.at[step, cut],
            device_id={"group": source},
            device_id_type=MESH,
        ).wait_recv()

    def hop(way, block, piece, target):
        return pltpu.make_async_remote_copy(
            src_ref=out.at[block, piece],
            dst_ref=out.at[block, piece],
            send_sem=send.at[way, block, piece],
            recv_sem=recv.at[block, piece],
            device_id={"expert": target},
            device_id_type=MESH,
        )

    def hop_up(block, piece):
        return hop(0, block, piece, me + LANES)

    def hop_down(block, piece):
        return hop(1, block, piece, me - LANES)

    def hop_side(block, piece):
        return hop(2, block, piece, beside)

    steps = [(step, cut) for step in range(groups) for cut in range(CUTS)]
    away = steps[CUTS:]
    for step, cut in away:
        pair_copy(step, cut).start()
    stay = pl.ds(my_group * CUTS, CUTS)
    own = pltpu.make_async_copy(leaving.at[stay], out.at[me, stay], own_sem)
    own.start()
    own.wait()

    def visit(reach, act, arrive):
        for step, cut in steps:
            def above(block, piece):
                arrive(block, piece)
                pl.when(line > 0)(lambda: act(hop_down(block, piece)))
                act(hop_side(block, piece))

            def below(block, piece):
                arrive(block, piece)
                pl.when(line < lines - 1)(lambda: act(hop_up(block, piece)))
                act(hop_side(block, piece))

            piece = lax.rem(my_group + groups - step, groups) * CUTS + cut
            pl.when(line - reach >= 0)(functools.partial(below, me - reach * LANES, piece))
            pl.when(line + reach <= lines - 1)(
                functools.partial(above, me + reach * LANES, piece)
            )

    def visit_own(step, cut, act):
        piece = lax.rem(my_group + groups - step, groups) * CUTS + cut
        act(hop_side(me, piece))
        pl.when(line < lines - 1)(lambda: act(hop_up(me, piece)))
        pl.when(line > 0)(lambda: act(hop_down(me, piece)))

    def begin(copy):
        copy.start()

    def sent(copy):
        copy.wait_send()

    for step, cut in steps:
        if step:
            pair_wait(step, cut)
        visit_own(step, cut, begin)
    for reach in range(1, lines):
        visit(reach, begin, lambda block, piece: hop_side(block, piece).wait_recv())
    for place in range(lines):
        for piece in range(groups * CUTS):
            hop_side(place * LANES + 1 - lane, piece).wait_recv()
    for step, cut in steps:
        visit_own(step, cut, sent)
    for reach in range(1, lines):
        visit(reach, sent, lambda block, piece: None)
    for step, cut in away:
        pair_copy(step, cut).wait_send()


def reduce_kernel(
    groups, members, parts, home, side, up, down, passing, total,
    pair_send, pair_recv, side_send, side_recv, line_send, up_recv, down_recv,
):
    lines = members // LANES
    my_group = lax.axis_index("group")
    me = lax.axis_index("expert")
    line, lane = me // LANES, lax.rem(me, LANES)
    beside = line * LANES + 1 - lane
    greet(groups, me, lines)

    def side_copy(place, piece):
        return pltpu.make_async_remote_copy(
            src_ref=parts.at[place * LANES + 1 - lane, piece],
            dst_ref=side.at[place, piece],
            send_sem=side_send.at[place, piece],
            recv_sem=side_recv.at[place, piece],
            device_id={"expert": beside},
            device_id_type=MESH,
        )

    def line_copy(land, recv, place, piece, target):
        return pltpu.make_async_remote_copy(
            src_ref=passing.at[place, piece],
            dst_ref=land.at[place, piece],
            send_sem=line_send.at[place, piece],
            recv_sem=recv.at[place, piece],
            device_id={"expert": target},
            device_id_type=MESH,
        )

    def up_copy(place, piece):
        return line_copy(up, up_recv, place, piece, me + LANES)

    def down_copy(place, piece):
        return line_copy(down, down_recv, place, piece, me - LANES)

    steps = [(step, cut) for step in range(1, groups + 1) for cut in range(CUTS)]
    away = steps[:-CUTS]

    def far_first(above, below):
        for reach in range(lines - 1, 0, -1):
            for step, cut in steps:
                piece = lax.rem(my_group + step, groups) * CUTS + cut
                pl.when(line + reach <= lines - 1)(
                    functools.partial(above, line + reach, piece)
                )
                pl.when(line - reach >= 0)(functools.partial(below, line - reach, piece))

    def begin(place, piece):
        side_copy(place, piece).start()

    far_first(begin, begin)
    for step, cut in steps:
        begin(line, lax.rem(my_group + step, groups) * CUTS + cut)

    def pair_sum(place, piece):
        mine = parts[place * LANES + lane, piece].astype(jnp.float32)
        return mine + side[place, piece].astype(jnp.float32)

    def pass_on(land, copy_of, has_before, place, piece):
        side_copy(place, piece).wait_recv()

        @pl.when(has_before)
        def _():
            copy_of(place, piece).wait_recv()
            both = pair_sum(place, piece) + land[place, piece].astype(jnp.float32)
            passing[place, piece] = both.astype(passing.dtype)

        @pl.when(jnp.logical_not(has_before))
        def _():
            passing[place, piece] = pair_sum(place, piece).astype(passing.dtype)

        copy_of(place, piece).start()

    far_first(
        functools.partial(pass_on, up, up_copy, line > 0),
        functools.partial(pass_on, down, down_copy, line < lines - 1),
    )

    def pair_copy(step, cut):
        other = lax.rem(my_group + step, groups)
        return pltpu.make_async_remote_copy(
            src_ref=passing.at[line, other * CUTS + cut],
            dst_ref=home.at[my_group * CUTS + cut],
            send_sem=pair_send.at[step, cut],
            recv_sem=pair_recv.at[step, cut],
            device_id={"group": other},
            device_id_type=MESH,
        )

    for step, cut in steps:
        piece = lax.rem(my_group + step, groups) * CUTS + cut
        side_copy(line, piece).wait_recv()
        total[...] = pair_sum(line, piece)

        @pl.when(line > 0)
        def _():
            up_copy(line, piece).wait_recv()
            total[...] += up[line, piece].astype(jnp.float32)

        @pl.when(line < lines - 1)
        def _():
            down_copy(line, piece).wait_recv()
            total[...] += down[line, piece].astype(jnp.float32)

        if step < groups:
            passing[line, piece] = total[...].astype(passing.dtype)
            pair_copy(step, cut).start()
        else:
            home[my_group * CUTS + cut] = total[...].astype(home.dtype)
    for step, cut in away:
        source = lax.rem(my_group + groups - step, groups)
        pltpu.make_async_remote_copy(
            src_ref=passing.at[line, source * CUTS + cut],
            dst_ref=home.at[source * CUTS + cut],
            send_sem=pair_send.at[step, cut],
            recv_sem=pair_recv.at[step, cut],
            device_id={"group": source},
            device_id_type=MESH,
        ).wait_recv()
        pair_copy(step, cut).wait_send()
    far_first(
        lambda place, piece: up_copy(place, piece).wait_send(),
        lambda place, piece: down_copy(place, piece).wait_send(),
    )
    for place in range(lines):
        for piece in range(groups * CUTS):
            side_copy(place, piece).wait_send()


def comm_cost(array, members):
    return pl.CostEstimate(
        flops=0, bytes_accessed=32 * members * array.size * 2 // 2, transcendentals=0
    )


def gather_rows(leaving, members):
    groups, visitors, features = leaving.shape
    leaving = leaving.reshape(groups * CUTS, visitors // CUTS, features)
    dma = pltpu.SemaphoreType.DMA
    return pl.pallas_call(
        functools.partial(gather_kernel, groups, members),
        out_shape=jax.ShapeDtypeStruct((members, *leaving.shape), leaving.dtype),
        in_specs=[pl.BlockSpec(memory_space=pltpu.VMEM)],
        out_specs=pl.BlockSpec(memory_space=pltpu.VMEM),
        scratch_shapes=[
            dma(()),
            dma((groups, CUTS)), dma((groups, CUTS)),
            dma((3, members, groups * CUTS)), dma((members, groups * CUTS)),
        ],
        compiler_params=pltpu.CompilerParams(
            collective_id=0, has_side_effects=True, vmem_limit_bytes=8 << 20
        ),
        cost_estimate=comm_cost(leaving, members),
        name="gather_rows",
    )(leaving)


def reduce_rows(parts, groups, members):
    pieces = groups * CUTS
    block = (pieces, parts.shape[0] // (pieces * members), parts.shape[1])
    lines = members // LANES
    dma = pltpu.SemaphoreType.DMA
    slots = pltpu.VMEM((lines, *block), parts.dtype)
    return pl.pallas_call(
        functools.partial(reduce_kernel, groups, members),
        out_shape=jax.ShapeDtypeStruct(block, parts.dtype),
        in_specs=[pl.BlockSpec(memory_space=pltpu.VMEM)],
        out_specs=pl.BlockSpec(memory_space=pltpu.VMEM),
        scratch_shapes=[
            slots, slots, slots, slots, pltpu.VMEM(block[1:], jnp.float32),
            dma((groups, CUTS)), dma((groups, CUTS)), *[dma((lines, pieces))] * 5,
        ],
        compiler_params=pltpu.CompilerParams(
            collective_id=1, has_side_effects=True, vmem_limit_bytes=12 << 20
        ),
        cost_estimate=comm_cost(parts, 1),
        name="reduce_rows",
    )(parts.reshape(members, *block))


def dense_device(tokens, grad_out, expert_ids, gate_score, w_gate_up, w_down):
    groups = lax.axis_size("group")
    members = lax.axis_size("expert")
    shares = lax.axis_size("dp")
    my_group = lax.axis_index("group")
    my_index = lax.axis_index("expert")
    per_column, features = tokens.shape
    visitors = per_column // groups
    arrivals = groups * visitors
    expert_rows = members * arrivals
    top_count = expert_ids.shape[1]
    weights = route_weights(gate_score)
    my_expert = my_group * members + my_index
    share = jnp.sum(jnp.where(expert_ids == my_expert, weights, 0.0), axis=1)
    token_group = (expert_ids[:, 0] // members).reshape(groups, members, per_column)
    here = token_group == my_group
    arrival_table = slot_matrix(here[..., None], visitors)[:, :, 0]
    row_share = jnp.sum(
        arrival_table * share.reshape(groups, members, 1, per_column), axis=3
    )
    row_share = jnp.transpose(row_share, (1, 0, 2)).reshape(expert_rows, 1)
    group_range = jnp.arange(groups, dtype=jnp.int32)
    visits_mine = token_group[my_group, my_index][:, None] == group_range
    leave_table = slot_matrix(visits_mine, visitors).astype(jnp.bfloat16)
    gate_weights = w_gate_up[0]
    down_weights = w_down[0]

    def dispatch(values):
        leaving = jnp.einsum(
            "gst,tf->gsf", leave_table, values, preferred_element_type=jnp.float32
        ).astype(jnp.bfloat16)
        return gather_rows(leaving, members).reshape(expert_rows, features)

    rows_in = dispatch(tokens)
    rows_grad = dispatch(grad_out)

    swap = [(i, (i + 1) % shares) for i in range(shares)]

    def dp_sum(value):
        total = value
        moving = value.astype(jnp.bfloat16)
        for _ in range(shares - 1):
            moving = lax.ppermute(moving, "dp", swap)
            total = total + moving.astype(jnp.float32)
        return total

    gate_both = dp_sum(
        jnp.einsum("rf,fkh->rkh", rows_in, gate_weights, preferred_element_type=jnp.float32)
    )
    grad_sum = dp_sum(
        jnp.einsum("rf,hf->rh", rows_grad, down_weights, preferred_element_type=jnp.float32)
    )
    gate_pre = gate_both[:, 0]
    up_pre = gate_both[:, 1]
    hidden = (jax.nn.silu(gate_pre) * up_pre).astype(jnp.bfloat16)
    expert_out = jnp.dot(hidden, down_weights, preferred_element_type=jnp.float32)
    out_part = (expert_out * row_share).astype(jnp.bfloat16)
    pre_grad = local_grad(gate_pre, up_pre, grad_sum * row_share)
    grad_part = jnp.einsum(
        "rkh,fkh->rf", pre_grad, gate_weights, preferred_element_type=jnp.float32
    ).astype(jnp.bfloat16)

    def give_back(parts):
        home = reduce_rows(parts, groups, members).reshape(groups, visitors, features)
        return jnp.einsum(
            "gst,gsf->tf", leave_table, home, preferred_element_type=jnp.float32
        ).astype(jnp.bfloat16)

    return (give_back(out_part), give_back(grad_part))


def on_device(tokens, grad_out, expert_ids, gate_score, w_gate_up, w_down):
    groups = lax.axis_size("group")
    members = lax.axis_size("expert")
    my_group = lax.axis_index("group")
    my_index = lax.axis_index("expert")
    per_column = tokens.shape[0]
    features = tokens.shape[1]
    visitors = per_column // 2
    top_count = expert_ids.shape[1]
    arrivals = groups * visitors
    capacity = min(arrivals, (3 * per_column * top_count + 2 * members - 1) // (2 * members))
    expert_rows = members * capacity
    weights = route_weights(gate_score).reshape(groups, members, per_column, top_count)
    pick_ids = expert_ids.reshape(groups, members, per_column, top_count)
    group_range = jnp.arange(groups, dtype=jnp.int32)
    my_picks = pick_ids[my_group, my_index]
    visits_mine = jnp.any(my_picks[:, :, None] // members == group_range, axis=1)
    leave_table = slot_matrix(visits_mine, visitors).astype(jnp.bfloat16)
    visits_here = jnp.any(pick_ids // members == my_group, axis=3)
    arrival_table = slot_matrix(visits_here[..., None], visitors)[:, :, 0]
    row_ids = jnp.einsum(
        "gest,getk->gesk", arrival_table, pick_ids.astype(jnp.float32), precision=HIGHEST
    )
    row_weights = jnp.einsum("gest,getk->gesk", arrival_table, weights, precision=HIGHEST)
    targets = (my_group * members + jnp.arange(members, dtype=jnp.int32)).astype(jnp.float32)
    matched = row_ids[..., None] == targets
    picked = jnp.any(matched, axis=3)
    picked_weight = jnp.sum(jnp.where(matched, row_weights[..., None], 0.0), axis=3)
    send_flags = picked[:, my_index].reshape(arrivals, members)
    send_table = slot_matrix(send_flags, capacity)
    send_share = jnp.transpose(picked_weight[:, my_index].reshape(arrivals, members))
    send_weight = send_table * send_share[:, None, :]
    came_flags = jnp.transpose(picked[:, :, :, my_index], (1, 0, 2)).reshape(members, arrivals)
    came_table = slot_matrix(came_flags[..., None], capacity)[:, 0]
    came_share = jnp.transpose(picked_weight[:, :, :, my_index], (1, 0, 2)).reshape(
        members, arrivals
    )
    slot_weight = jnp.einsum("ecr,er->ec", came_table, came_share, precision=HIGHEST).reshape(
        expert_rows
    )

    def dispatch(values):
        leaving = jnp.einsum(
            "gst,tf->gsf", leave_table, values, preferred_element_type=jnp.float32
        ).astype(jnp.bfloat16)
        arrived = across(leaving).reshape(arrivals, features)
        onward = jnp.einsum(
            "ecr,rf->ecf",
            send_table.astype(jnp.bfloat16),
            arrived,
            preferred_element_type=jnp.float32,
        ).astype(jnp.bfloat16)
        return within(onward).reshape(expert_rows, features)

    def combine(values, table):
        returned = within(values.reshape(members, capacity, features)).astype(jnp.float32)
        summed = jnp.einsum("ecr,ecf->rf", table, returned, precision=HIGHEST).astype(jnp.bfloat16)
        home = across(summed.reshape(groups, visitors, features))
        return jnp.einsum(
            "gst,gsf->tf", leave_table, home, preferred_element_type=jnp.float32
        ).astype(jnp.bfloat16)

    rows_in = dispatch(tokens)
    rows_grad = dispatch(grad_out)
    gate_weights = w_gate_up[0]
    down_weights = w_down[0]
    partial_value = jnp.einsum(
        "rf,fkh->rkh", rows_in, gate_weights, preferred_element_type=jnp.float32
    )
    grad_partial = jnp.einsum(
        "rf,hf->rh", rows_grad, down_weights, preferred_element_type=jnp.float32
    )
    empty_rows = jnp.zeros((expert_rows, features), jnp.float32)
    gate_both = share_sum(partial_value)
    gate_pre = gate_both[:, 0]
    up_pre = gate_both[:, 1]
    hidden = (jax.nn.silu(gate_pre) * up_pre).astype(jnp.bfloat16)[:, None, :]

    def down_step(running_sum, gathered, first_row):
        return jnp.dot(gathered[:, 0], down_weights, preferred_element_type=jnp.float32)

    expert_out = share_fold(hidden, down_step, empty_rows).astype(jnp.bfloat16)
    hidden_grad = share_sum(grad_partial[:, None, :])[:, 0] * slot_weight[:, None]
    pre_grad = local_grad(gate_pre, up_pre, hidden_grad)

    def input_step(running_sum, gathered, first_row):
        return jnp.einsum("rkh,fkh->rf", gathered, gate_weights, preferred_element_type=jnp.float32)

    expert_grad = share_fold(pre_grad, input_step, empty_rows).astype(jnp.bfloat16)
    layer_out = combine(expert_out, send_weight)
    grad_in = combine(expert_grad, send_table)
    return (layer_out, grad_in)


def per_device(tokens, grad_out, expert_ids, gate_score, w_gate_up, w_down):
    members = lax.axis_size("expert")
    dense = expert_ids.shape[1] == members and members % LANES == 0
    plan = dense_device if dense else on_device
    return plan(tokens, grad_out, expert_ids, gate_score, w_gate_up, w_down)


def solution(mesh):
    return jax.shard_map(
        per_device,
        mesh=mesh,
        in_specs=(
            P(("group", "expert"), "dp"),
            P(("group", "expert"), "dp"),
            P(),
            P(),
            P(("group", "expert"), "dp", None, None),
            P(("group", "expert"), None, "dp"),
        ),
        out_specs=(P(("group", "expert"), "dp"), P(("group", "expert"), "dp")),
        check_vma=False,
    )
```

profile of v0, /device:TPU:1, one launch (start us, length us, event | category | flops | bytes accessed | tf_op | source)
XLA Modules:
  0.0 105.6 jit_solution(10150103226068172068)
XLA Ops:
  0.6 0.0 copy-start
  0.6 0.8 slice_reduce_fusion
  1.4 0.1 squeeze.19
  1.5 0.1 fusion.41
  1.6 0.1 reduce_window_sum.22
  1.7 0.1 copy.14
  1.8 0.0 copy-done
  1.8 0.2 convolution_convert_fusion.1
  1.9 0.0 slice-start.3
  2.0 19.3 %gather_rows.2 = bf16[8,4,8,2560]{3,2,1,0:T(8,128)(2,1)S(1)} custom-call(bf16[4,8,2560]{2,1,0:T(8,128)(2,1)S(1)} %bitcast.104), custom_call_target="tpu_custom_call" | custom-call | bytes 20971520 | tf_op jit(solution)/shard_map/gather_rows/pallas_call | solution.py:323
  21.3 0.0 copy-start.1
  21.3 0.0 slice-start.4
  21.3 8.4 %fusion.57 = (bf16[256,2,1024]{2,0,1:T(8,128)(2,1)}, f32[256,2,1024]{2,0,1:T(8,128)S(1)}) fusion(bf16[256,2560,1]{1,0,2:T(8,128)(2,1)S(1)} %bitcast.98, bf16[2560,2,1024]{2,1,0:T(2,128)(2,1)} %bitcast.107), kind=kOutput, calls=%fused_computation.78 | convolution fusion | flops 2684878848 | bytes 14942208 | tf_op jit(solution)/shard_map/rf,fkh->rkh/dot_general | solution.py:411
  29.7 1.2 %collective-permute-start = (bf16[256,2,1024]{2,0,1:T(8,128)(2,1)}, bf16[256,2,1024]{2,0,1:T(8,128)(2,1)}, u32[]{:S(2)}, u32[]{:S(2)}) collective-permute-start(bf16[256,2,1024]{2,0,1:T(8,128)(2,1)} %get-tuple-element.7), channel_id=1, source_target_pairs={{0,1},{1,0},{2,3},{3,2},{4,5},{5,4},{6,7},{7,6},{8,9},{9,8},{10,11... | collective-permute-start | bytes 3145736 | tf_op jit(solution)/shard_map/ppermute | solution.py:406
  31.0 0.0 copy-done.1
  31.0 0.2 convolution_convert_fusion
  31.1 18.9 %gather_rows.3 = bf16[8,4,8,2560]{3,2,1,0:T(8,128)(2,1)S(1)} custom-call(bf16[4,8,2560]{2,1,0:T(8,128)(2,1)S(1)} %bitcast.105), custom_call_target="tpu_custom_call" | custom-call | bytes 20971520 | tf_op jit(solution)/shard_map/gather_rows/pallas_call | solution.py:323
  50.0 0.0 slice-done.3
  50.1 0.0 slice-done.4
  50.1 0.0 copy-start.2
  50.1 0.0 copy-start.3
  50.1 2.4 %fusion.58 = (bf16[256,1024]{1,0:T(8,128)(2,1)}, f32[256,1024]{1,0:T(8,128)S(1)}) fusion(bf16[256,2560]{1,0:T(8,128)(2,1)S(1)} %bitcast.99, bf16[1,1024,2560]{2,1,0:T(8,128)(2,1)S(1)} %bitcast.112), kind=kOutput, calls=%fused_computation.79 | convolution fusion | flops 1342439424 | bytes 8126464 | tf_op jit(solution)/shard_map/rf,hf->rh/dot_general | solution.py:414
  52.5 0.3 collective-permute-start.1
  52.7 0.0 copy-done.2
  52.8 0.0 copy-done.3
  52.8 0.1 mul.69
  52.9 0.4 reduce_window_sum.23
  53.3 0.1 select_reduce_fusion
  53.4 0.1 mul.72
  53.5 0.0 collective-permute-done
  53.5 0.0 slice-start
  53.5 1.7 %convert_add_fusion = f32[256,2,1024]{2,0,1:T(8,128)S(1)} fusion(f32[256,2,1024]{2,0,1:T(8,128)S(1)} %get-tuple-element.8, bf16[256,2,1024]{2,0,1:T(8,128)(2,1)} %collective-permute-done), kind=kLoop, calls=%fused_computation.18 | loop fusion | flops 1048576 | bytes 5242880 | tf_op jit(solution)/shard_map/add | solution.py:407
  55.2 0.0 slice-start.1
  55.3 0.0 slice-start.2
  55.3 4.2 %fusion.17 = bf16[256,2560]{1,0:T(8,128)(2,1)S(1)} fusion(bf16[1,1024,2560]{2,1,0:T(8,128)(2,1)} %param.11, f32[256]{0:T(256)S(1)} %mul.72, f32[256,2,1024]{2,0,1:T(8,128)S(1)} %convert_add_fusion), kind=kOutput, calls=%fused_computation.11 | convolution fusion | flops 1345060864 | bytes 8651776 | tf_op jit(solution)/shard_map/dot_general | solution.py:419
  59.5 19.9 %reduce_rows.2 = bf16[4,8,2560]{2,1,0:T(8,128)(2,1)S(1)} custom-call(bf16[8,4,8,2560]{3,2,1,0:T(8,128)(2,1)S(1)} %bitcast.101), custom_call_target="tpu_custom_call" | custom-call | bytes 20971520 | tf_op jit(solution)/shard_map/reduce_rows/pallas_call | solution.py:347
  79.4 0.9 fusion.20
  80.3 0.0 collective-permute-done.1
  80.3 1.7 %fusion.36 = (bf16[256,1,1024]{2,0,1:T(8,128)(2,1)S(1)}, bf16[256,1,1024]{2,0,1:T(8,128)(2,1)S(1)}) fusion(f32[256,2,1024]{2,0,1:T(8,128)S(1)} %convert_add_fusion, f32[256]{0:T(256)S(1)} %mul.72, f32[256,1024]{1,0:T(8,128)S(1)} %get-tuple-element.10, bf16[256,1024]{1,0:T(8,128)(2,1)} %collective-permute-done.1), kind=kLoop, calls=%fused_computation.39 | loop fusion | flops 4194304 | bytes 4719616 | tf_op jit(solution)/shard_map/stack | solution.py:29
  82.0 0.0 slice-done
  82.0 0.0 slice-done.1
  82.0 0.0 slice-done.2
  82.0 3.6 %fusion.14 = bf16[256,2560]{1,0:T(8,128)(2,1)S(1)} fusion(bf16[2560,2,1024]{2,1,0:T(2,128)(2,1)S(1)} %bitcast.110, bf16[256,1,1024]{2,0,1:T(8,128)(2,1)S(1)} %get-tuple-element.6, bf16[256,1,1024]{2,0,1:T(8,128)(2,1)S(1)} %get-tuple-element.5), kind=kOutput, calls=%fused_computation.10 | convolution fusion | flops 2685534208 | bytes 12845056 | tf_op jit(solution)/shard_map/rkh,fkh->rf/dot_general | solution.py:422
  85.6 19.0 %reduce_rows.3 = bf16[4,8,2560]{2,1,0:T(8,128)(2,1)S(1)} custom-call(bf16[8,4,8,2560]{3,2,1,0:T(8,128)(2,1)S(1)} %bitcast.100), custom_call_target="tpu_custom_call" | custom-call | bytes 20971520 | tf_op jit(solution)/shard_map/reduce_rows/pallas_call | solution.py:347
  104.7 0.9 fusion.21
  (10 shorter events, 0.1 us)
Async XLA Ops:
  0.6 1.1 %copy-start = (bf16[32,2560]{1,0:T(8,128)(2,1)S(1)}, bf16[32,2560]{1,0:T(8,128)(2,1)}, u32[]{:S(2)}) copy-start(bf16[32,2560]{1,0:T(8,128)(2,1)} %param.6) | copy-start | bytes 491524
  1.9 48.1 %slice-start.3 = ((s8[5242880]{0:T(1024)(128)(4,1)}), s8[4194304]{0:T(1024)(128)(4,1)S(1)}, s32[]{:S(2)}) async-start(s8[5242880]{0:T(1024)(128)(4,1)} %bitcast.111), calls=%async_computation.3 | async-start | bytes 8388608
  21.3 9.7 %copy-start.1 = (bf16[32,2560]{1,0:T(8,128)(2,1)S(1)}, bf16[32,2560]{1,0:T(8,128)(2,1)}, u32[]{:S(2)}) copy-start(bf16[32,2560]{1,0:T(8,128)(2,1)} %param.7) | copy-start | bytes 491524
  21.3 28.8 %slice-start.4 = ((s8[5242880]{0:T(1024)(128)(4,1)}), s8[1048576]{0:T(1024)(128)(4,1)S(1)}, s32[]{:S(2)}) async-start(s8[5242880]{0:T(1024)(128)(4,1)} %bitcast.111), calls=%async_computation.4 | async-start | bytes 2097152
  29.7 23.7 %collective-permute-start = (bf16[256,2,1024]{2,0,1:T(8,128)(2,1)}, bf16[256,2,1024]{2,0,1:T(8,128)(2,1)}, u32[]{:S(2)}, u32[]{:S(2)}) collective-permute-start(bf16[256,2,1024]{2,0,1:T(8,128)(2,1)} %get-tuple-element.7), channel_id=1, source_target_pairs={{0,1},{1,0},{2,3},{3,2},{4,5},{5,4},{6,7},{7,6},{8,9},{9,8},{10,11... | collective-permute-start | bytes 3145736 | tf_op jit(solution)/shard_map/ppermute | solution.py:406
  50.1 2.7 %copy-start.2 = (f32[512,8]{0,1:T(8,128)S(1)}, f32[512,8]{0,1:T(8,128)}, u32[]{:S(2)}) copy-start(f32[512,8]{0,1:T(8,128)} %param.9) | copy-start | bytes 49156
  50.1 2.7 %copy-start.3 = (s32[512,8]{0,1:T(8,128)S(1)}, s32[512,8]{0,1:T(8,128)}, u32[]{:S(2)}) copy-start(s32[512,8]{0,1:T(8,128)} %param.8) | copy-start | bytes 49156
  52.5 27.8 %collective-permute-start.1 = (bf16[256,1024]{1,0:T(8,128)(2,1)}, bf16[256,1024]{1,0:T(8,128)(2,1)}, u32[]{:S(2)}, u32[]{:S(2)}) collective-permute-start(bf16[256,1024]{1,0:T(8,128)(2,1)} %get-tuple-element.9), channel_id=1, source_target_pairs={{0,1},{1,0},{2,3},{3,2},{4,5},{5,4},{6,7},{7,6},{8,9},{9,8},{10,11... | collective-permute-start | bytes 1572872 | tf_op jit(solution)/shard_map/ppermute | solution.py:406
  53.5 28.5 %slice-start = ((s8[10485760]{0:T(1024)(128)(4,1)}), s8[4194304]{0:T(1024)(128)(4,1)S(1)}, s32[]{:S(2)}) async-start(s8[10485760]{0:T(1024)(128)(4,1)} %bitcast.108), calls=%async_computation | async-start | bytes 8388608
  55.2 26.7 %slice-start.1 = ((s8[10485760]{0:T(1024)(128)(4,1)}), s8[4194304]{0:T(1024)(128)(4,1)S(1)}, s32[]{:S(2)}) async-start(s8[10485760]{0:T(1024)(128)(4,1)} %bitcast.108), calls=%async_computation.1 | async-start | bytes 8388608
  55.3 26.7 %slice-start.2 = ((s8[10485760]{0:T(1024)(128)(4,1)}), s8[2097152]{0:T(1024)(128)(4,1)S(1)}, s32[]{:S(2)}) async-start(s8[10485760]{0:T(1024)(128)(4,1)} %bitcast.108), calls=%async_computation.2 | async-start | bytes 4194304
where the time goes:
time: 107 us; the launch traced here: 106 us
  Pallas kernels  77.2 us (72%)
  matrix products  20.7 us (19%)
  other arithmetic  4.15 us (4%)
  starting transfers between devices  1.47 us (1%)
  local copies, waits for them, and re-layouts  1.17 us (1%)
    pallas_call x2, Pallas kernels, reduce_rows(): pl.pallas_call(functools.partial(reduce_kernel, groups, members), out_sha...  38.9 us
    pallas_call x2, Pallas kernels, gather_rows(): pl.pallas_call(functools.partial(gather_kernel, groups, members), out_sha...  38.2 us
    dot_general x1, matrix products, dense_device(): jnp.einsum('rf,fkh->rkh', rows_in, gate_weights, preferred_element_type=j...  8.43 us
    dot_general x1, matrix products, dense_device(): jnp.dot(hidden, down_weights, preferred_element_type=jnp.float32)  4.19 us
    dot_general x1, matrix products, dense_device(): jnp.einsum('rkh,fkh->rf', pre_grad, gate_weights, preferred_element_type=...  3.6 us
    dot_general x1, matrix products, dense_device(): jnp.einsum('rf,hf->rh', rows_grad, down_weights, preferred_element_type=j...  2.37 us
  transfers between devices with their start and end apart: 2, of which 0 were waited for; matrix products, arithmetic and copies ran while one was open for 10% of the time, Pallas kernels for 37%

commit v1 on v0

v1 whole, which is shorter than its diff:
```python
import functools

import jax
import jax.numpy as jnp
from jax import lax
from jax.experimental import pallas as pl
from jax.experimental.pallas import tpu as pltpu
from jax.sharding import PartitionSpec as P

HIGHEST = lax.Precision.HIGHEST


def route_weights(gate_score):
    sigmoid_score = jax.nn.sigmoid(gate_score)
    return 2.5 * sigmoid_score / jnp.sum(sigmoid_score, axis=1, keepdims=True)


def slot_matrix(marked, places):
    count = marked.shape[-2]
    order = jnp.arange(count, dtype=jnp.int32)
    earlier = (order[:, None] >= order[None, :]).astype(jnp.bfloat16)
    running = jnp.einsum(
        "ij,...jk->...ik",
        earlier,
        marked.astype(jnp.bfloat16),
        preferred_element_type=jnp.float32,
    )
    slot_range = jnp.arange(1, places + 1, dtype=jnp.int32).astype(jnp.float32)
    matched = marked[..., None] & (running[..., None] == slot_range)
    return jnp.moveaxis(matched, -3, -1).astype(jnp.float32)


def local_grad(gate_pre, up_pre, hidden_grad):
    sigmoid_gate = jax.nn.sigmoid(gate_pre)
    gate_grad = hidden_grad * up_pre * sigmoid_gate * (1.0 + gate_pre * (1.0 - sigmoid_gate))
    up_grad = hidden_grad * gate_pre * sigmoid_gate
    return jnp.stack([gate_grad, up_grad], axis=1).astype(jnp.bfloat16)


def across(blocks):
    return lax.all_to_all(blocks, "group", split_axis=0, concat_axis=0, tiled=True)


def within(blocks):
    return lax.all_to_all(blocks, "expert", split_axis=0, concat_axis=0, tiled=True)


def share_sum(partial_value):
    return lax.psum_scatter(partial_value, "dp", scatter_dimension=2, tiled=True)


def share_fold(shares, step_fn, start_value):
    return step_fn(start_value, lax.all_gather(shares, "dp", axis=2, tiled=True), jnp.int32(0))


MESH = pl.DeviceIdType.MESH
LANES = 2
TILE = 256
STRIP = 16
HALVES = 2
LINES = 4
SCHEDULE = (
    ("gather", 0, 0, 0),
    ("separate", 0),
    ("gather", 0, 0, 1),
    ("gather", 1, 0, 1),
    ("separate", 1),
    ("gather", 0, 1, 0),
    ("separate", 2),
    ("separate", 3),
    ("gather", 0, 1, 1),
    ("gather", 0, 2, 1),
    ("gather", 1, 0, 0),
    ("separate", 4),
    ("gather", 1, 1, 1),
    ("multiply_in", 0, 0),
    ("gather", 0, 2, 0),
    ("multiply_in", 0, 1),
    ("gather", 0, 3, 0),
    ("gather", 0, 3, 1),
    ("gather", 1, 1, 0),
    ("gather", 1, 2, 0),
    ("gather", 1, 3, 1),
    ("multiply_in", 1, 0),
    ("gather", 1, 3, 0),
    ("activate_out", 0),
    ("multiply_out", 0, 0),
    ("multiply_in", 1, 1),
    ("multiply_out", 0, 1),
    ("multiply_grad", 0),
    ("gather", 1, 2, 1),
    ("give_back", 0, 1, 1),
    ("give_back", 0, 1, 0),
    ("activate_out", 1),
    ("multiply_out", 1, 0),
    ("multiply_grad", 1),
    ("multiply_out", 1, 1),
    ("give_back", 0, 3, 0),
    ("activate_back", 0),
    ("give_back", 0, 2, 0),
    ("multiply_back", 0, 0),
    ("give_back", 0, 3, 1),
    ("multiply_back", 0, 1),
    ("give_back", 0, 2, 1),
    ("activate_back", 1),
    ("give_back", 1, 1, 0),
    ("multiply_back", 1, 0),
    ("finish", 0, 0),
    ("give_back", 1, 1, 1),
    ("multiply_back", 1, 1),
    ("give_back", 1, 3, 0),
    ("give_back", 1, 2, 0),
    ("give_back", 1, 3, 1),
    ("give_back", 1, 2, 1),
    ("finish", 0, 1),
    ("finish", 1, 0),
    ("finish", 1, 1),
)


def visit_order(lines):
    orders = []
    for line in range(lines):
        orders.append(sorted(range(lines), key=lambda level: (abs(level - line), level)))
    for line in range(lines // 2, lines):
        orders[line] = [lines - 1 - level for level in orders[lines - 1 - line]]
    return orders


def layer_kernel(
    tokens, grad_out, ids, scores, gate_hbm, down_hbm,
    layer_out, grad_in,
    stage, weights, down, leaving, rows, own_pre, own_grad, out_pre, out_grad, in_pre, in_grad,
    hidden, pre, parts, side, land, passing, leaving_core, home, share, place_table,
    stage_sem, down_sem, pair_send, pair_recv, row_send, row_recv,
    pre_send, pre_recv, grad_send, grad_recv,
    side_send, side_recv, land_send, land_recv, core_send, core_recv,
):
    my_group = lax.axis_index("group")
    me = lax.axis_index("expert")
    my_share = lax.axis_index("dp")
    other = 1 - my_group
    line, lane = me // LANES, lax.rem(me, LANES)
    other_lane = 1 - lane
    beside = line * LANES + other_lane
    _, groups, visitors, features = leaving.shape
    per_column = tokens.shape[0]
    token_count = ids.shape[1]
    lines = side.shape[2]
    members = lines * LANES
    hidden_size = down.shape[0]
    half_lines = lines // HALVES
    half_members = half_lines * LANES
    block_rows = groups * visitors
    half_rows = half_members * block_rows
    half_features = features // HALVES
    my_half = line // half_lines
    orders = visit_order(lines)
    chunks = stage_sem.shape[0]

    def level_at(step):
        return sum(
            (line == place).astype(jnp.int32) * orders[place][step] for place in range(lines)
        )

    def remote(src, dst, send, recv, where):
        return pltpu.make_async_remote_copy(
            src_ref=src, dst_ref=dst, send_sem=send, recv_sem=recv,
            device_id=where, device_id_type=MESH,
        )

    chunk_rows = stage.shape[0] // chunks
    stage_copies = []
    for chunk in range(chunks):
        span = pl.ds(chunk * chunk_rows, chunk_rows)
        stage_copies.append(
            pltpu.make_async_copy(gate_hbm.at[span], stage.at[span], stage_sem.at[chunk])
        )
    down_copy = pltpu.make_async_copy(down_hbm, down, down_sem)

    barrier = pltpu.get_barrier_semaphore()

    def hello(where):
        pl.semaphore_signal(barrier, inc=1, device_id=where, device_id_type=MESH)

    hello({"group": other})
    hello({"expert": beside})
    hello({"dp": 1 - my_share})
    for step in range(1, lines):
        hello({"expert": level_at(step) * LANES + lane})
    for copy in stage_copies:
        copy.start()
    down_copy.start()

    def wide(value):
        return value.astype(jnp.float32)

    def half_dot(left, right):
        return jnp.dot(
            left.astype(jnp.bfloat16), right.astype(jnp.bfloat16),
            preferred_element_type=jnp.float32,
        )

    grouped = wide((ids[0:1, :] >= members).astype(jnp.int32))

    def token_iota(dimension):
        return lax.broadcasted_iota(jnp.int32, (token_count, token_count), dimension)

    before, after = token_iota(0), token_iota(1)
    together = jnp.logical_and(before // per_column == after // per_column, before < after)
    ranked = half_dot(
        jnp.concatenate([1.0 - grouped, grouped], axis=0), wide(together.astype(jnp.int32))
    )
    slot = jnp.where(grouped > 0.5, visitors + ranked[1:2], ranked[0:1])
    first_token = (my_group * members + me) * per_column
    token_of = lax.broadcasted_iota(jnp.int32, (token_count, per_column), 0)
    column_of = lax.broadcasted_iota(jnp.int32, (token_count, per_column), 1)
    own_slot = half_dot(slot, wide((token_of == first_token + column_of).astype(jnp.int32)))
    row_of = lax.broadcasted_iota(jnp.int32, (block_rows, per_column), 0)
    place_table[...] = wide((wide(row_of) == own_slot).astype(jnp.int32)).astype(jnp.bfloat16)
    for array, values in enumerate((tokens, grad_out)):
        moved = jnp.dot(
            place_table[...], values[...], preferred_element_type=jnp.float32
        ).astype(jnp.bfloat16)
        for group in range(groups):
            leaving[array, group] = moved[group * visitors:(group + 1) * visitors]
        rows[array, me, my_group] = leaving[array, my_group]

    pl.semaphore_wait(barrier, 3 + lines - 1)

    def pair_copy(array):
        return remote(
            leaving.at[array, other], rows.at[array, me, my_group],
            pair_send.at[array], pair_recv.at[array], {"group": other},
        )

    def pair_wait(array):
        remote(
            leaving.at[array, my_group], rows.at[array, me, other],
            pair_send.at[array], pair_recv.at[array], {"group": other},
        ).wait_recv()

    def hop(way, array, block, piece, target):
        where = rows.at[array, block, piece]
        return remote(
            where, where, row_send.at[way, array, block, piece],
            row_recv.at[array, block, piece], {"expert": target},
        )

    def hop_side(array, block, piece):
        return hop(0, array, block, piece, beside)

    has_up = line < lines - 1
    has_down = line > 0

    def forward(act, array, step, piece):
        level = level_at(step)
        block = level * LANES + lane
        pl.when(jnp.logical_and(level <= line, has_up))(
            lambda: act(hop(1, array, block, piece, me + LANES))
        )
        pl.when(jnp.logical_and(level >= line, has_down))(
            lambda: act(hop(2, array, block, piece, me - LANES))
        )
        act(hop_side(array, block, piece))

    def piece_at(index):
        return my_group if index == 0 else other

    def begin(copy):
        copy.start()

    def sent(copy):
        copy.wait_send()

    def gather(array, step, index):
        piece = piece_at(index)
        mine = level_at(step) * LANES + lane
        if step == 0:
            if index == 1:
                pair_wait(array)
        else:
            hop_side(array, mine, piece).wait_recv()
        forward(begin, array, step, piece)

    def gathered(array, stage_index):
        for step in range(stage_index * half_lines, (stage_index + 1) * half_lines):
            theirs = level_at(step) * LANES + other_lane
            for index in range(groups):
                hop_side(array, theirs, piece_at(index)).wait_recv()

    span_rows = STRIP * 2 * (hidden_size // 128)

    def separate(chunk):
        stage_copies[chunk].wait()
        to = lax.broadcasted_iota(jnp.int32, (span_rows, span_rows), 0)
        source = lax.broadcasted_iota(jnp.int32, (span_rows, span_rows), 1)
        per_row = span_rows // STRIP
        select = (source == lax.rem(to, STRIP) * per_row + to // STRIP).astype(jnp.bfloat16)
        passes = chunk_rows // (2 * span_rows)
        unroll = next(count for count in (8, 4, 2, 1) if passes % count == 0)

        def one(index, carry):
            at = chunk * passes + index
            first = pl.multiple_of(at * 2 * span_rows, 2 * span_rows)
            both = jnp.concatenate(
                [stage[pl.ds(first, span_rows)], stage[pl.ds(first + span_rows, span_rows)]],
                axis=1,
            )
            moved = jnp.dot(select, both, preferred_element_type=jnp.float32).astype(jnp.bfloat16)
            base = pl.multiple_of(at * 2 * STRIP, 2 * STRIP)
            for slot_at in range(per_row):
                column = (slot_at % 2) * hidden_size + (slot_at // 2) * 128
                for half in range(2):
                    weights[pl.ds(base + half * STRIP, STRIP), column:column + 128] = moved[
                        slot_at * STRIP:(slot_at + 1) * STRIP, half * 128:(half + 1) * 128
                    ]
            return carry

        lax.fori_loop(0, passes, one, 0, unroll=unroll)

    def half_at(stage_index):
        return my_half if stage_index == 0 else 1 - my_half

    def half_block(array, half):
        found = rows[array, pl.ds(half * half_members, half_members)]
        return found.reshape(half_rows, features)

    def tile_at(index):
        return pl.ds(pl.multiple_of(index * TILE, TILE), TILE)

    def pre_copy(stage_index, kind):
        columns = pl.ds(kind * hidden_size, hidden_size)
        return remote(
            out_pre.at[stage_index, :, columns], in_pre.at[stage_index, :, columns],
            pre_send.at[stage_index, kind], pre_recv.at[stage_index, kind],
            {"dp": 1 - my_share},
        )

    def grad_copy(stage_index):
        return remote(
            out_grad.at[stage_index], in_grad.at[stage_index],
            grad_send.at[stage_index], grad_recv.at[stage_index], {"dp": 1 - my_share},
        )

    def multiply_in(stage_index, kind):
        if kind == 0:
            gathered(0, stage_index)
        columns = pl.ds(kind * hidden_size, hidden_size)
        value = jnp.dot(
            half_block(0, half_at(stage_index)), weights[:, columns],
            preferred_element_type=jnp.float32,
        )
        own_pre[stage_index, :, columns] = value
        out_pre[stage_index, :, columns] = value.astype(jnp.bfloat16)
        pre_copy(stage_index, kind).start()

    def down_ready(stage_index):
        if stage_index == 0 and not waited:
            waited.append(True)
            down_copy.wait()

    waited = []

    def multiply_grad(stage_index):
        gathered(1, stage_index)
        down_ready(stage_index)
        value = lax.dot_general(
            half_block(1, half_at(stage_index)), down[...], (((1,), (1,)), ((), ())),
            preferred_element_type=jnp.float32,
        )
        own_grad[stage_index] = value
        out_grad[stage_index] = value.astype(jnp.bfloat16)
        grad_copy(stage_index).start()

    def make_share():
        score = jax.nn.sigmoid(scores[...])
        weight = 2.5 * score / jnp.sum(score, axis=0, keepdims=True)
        my_expert = my_group * members + me
        mine = jnp.sum(jnp.where(ids[...] == my_expert, weight, 0.0), axis=0, keepdims=True)
        token = lax.broadcasted_iota(jnp.int32, (1, token_count), 1)
        member = lax.rem(token // per_column, members)
        source = token // (per_column * members)
        rank = jnp.where(grouped > 0.5, ranked[1:2], ranked[0:1])
        row = wide(member * block_rows + source * visitors) + rank
        here = grouped == wide(my_group + jnp.zeros((1, token_count), jnp.int32))
        row = jnp.where(here, row, -1.0)
        at = wide(lax.broadcasted_iota(jnp.int32, (HALVES * half_rows, token_count), 0))
        share[...] = jnp.sum(jnp.where(at == row, mine, 0.0), axis=1, keepdims=True)

    def half_share(stage_index):
        first = pl.multiple_of(half_at(stage_index) * half_rows, half_rows)
        return share[pl.ds(first, half_rows), :]

    def put_parts(array, cut, stage_index, value):
        half = half_at(stage_index)
        parts[array, cut, pl.ds(half * half_members, half_members)] = value.astype(
            jnp.bfloat16
        ).reshape(half_members, block_rows, half_features)
        for step in range((stage_index + 1) * half_lines - 1, stage_index * half_lines - 1, -1):
            side_copy(array, step, cut).start()

    def activate_out(stage_index):
        if stage_index == 0:
            make_share()
        for kind in range(2):
            pre_copy(stage_index, kind).wait_recv()
        weight = half_share(stage_index)

        def one(index, carry):
            columns = tile_at(index)
            up_columns = tile_at(index + hidden_size // TILE)
            gate_pre = own_pre[stage_index, :, columns] + wide(in_pre[stage_index, :, columns])
            up_pre = own_pre[stage_index, :, up_columns] + wide(
                in_pre[stage_index, :, up_columns]
            )
            gate_sigmoid = jax.nn.sigmoid(gate_pre)
            gate_silu = gate_pre * gate_sigmoid
            hidden[:, columns] = (gate_silu * up_pre).astype(jnp.bfloat16)
            own_pre[stage_index, :, columns] = (
                weight * up_pre * gate_sigmoid * (1.0 + gate_pre * (1.0 - gate_sigmoid))
            )
            own_pre[stage_index, :, up_columns] = weight * gate_silu
            return carry

        lax.fori_loop(0, hidden_size // TILE, one, 0)

    def multiply_out(stage_index, cut):
        down_ready(stage_index)
        value = jnp.dot(
            hidden[...], down[:, cut * half_features:(cut + 1) * half_features],
            preferred_element_type=jnp.float32,
        )
        put_parts(0, cut, stage_index, value * half_share(stage_index))

    def activate_back(stage_index):
        grad_copy(stage_index).wait_recv()

        def one(index, carry):
            columns = tile_at(index)
            up_columns = tile_at(index + hidden_size // TILE)
            grad = own_grad[stage_index, :, columns] + wide(in_grad[stage_index, :, columns])
            pre[:, columns] = (grad * own_pre[stage_index, :, columns]).astype(jnp.bfloat16)
            pre[:, up_columns] = (grad * own_pre[stage_index, :, up_columns]).astype(
                jnp.bfloat16
            )
            return carry

        lax.fori_loop(0, hidden_size // TILE, one, 0)

    def multiply_back(stage_index, cut):
        value = lax.dot_general(
            pre[...], weights[cut * half_features:(cut + 1) * half_features, :],
            (((1,), (1,)), ((), ())), preferred_element_type=jnp.float32,
        )
        put_parts(1, cut, stage_index, value)

    def side_copy(array, step, cut):
        level = level_at(step)
        return remote(
            parts.at[array, cut, level * LANES + other_lane], side.at[array, cut, level],
            side_send.at[array, cut, level], side_recv.at[array, cut, level],
            {"expert": beside},
        )

    def land_copy(array, step, cut):
        return remote(
            passing.at[array, cut, step - 1], land.at[array, cut, line],
            land_send.at[array, cut, step - 1], land_recv.at[array, cut, line],
            {"expert": level_at(step) * LANES + lane},
        )

    def land_wait(array, step, cut):
        source = level_at(step)
        remote(
            passing.at[array, cut, step - 1], land.at[array, cut, source],
            land_send.at[array, cut, step - 1], land_recv.at[array, cut, source],
            {"expert": source * LANES + lane},
        ).wait_recv()

    def pair_sum(array, step, cut):
        side_copy(array, step, cut).wait_recv()
        level = level_at(step)
        return wide(parts[array, cut, level * LANES + lane]) + wide(side[array, cut, level])

    def give_back(array, step, cut):
        passing[array, cut, step - 1] = pair_sum(array, step, cut).astype(jnp.bfloat16)
        land_copy(array, step, cut).start()

    def cut_columns(cut):
        return pl.ds(cut * half_features, half_features)

    def core_copy(array, cut):
        return remote(
            leaving_core.at[array, cut, pl.ds(other * visitors, visitors)],
            home.at[array, my_group, :, cut_columns(cut)],
            core_send.at[array, cut], core_recv.at[array, cut], {"group": other},
        )

    def core_wait(array, cut):
        remote(
            leaving_core.at[array, cut, pl.ds(my_group * visitors, visitors)],
            home.at[array, other, :, cut_columns(cut)],
            core_send.at[array, cut], core_recv.at[array, cut], {"group": other},
        ).wait_recv()

    def finish(array, cut):
        total = pair_sum(array, 0, cut)
        for step in range(1, lines):
            land_wait(array, step, cut)
            total = total + wide(land[array, cut, level_at(step)])
        leaving_core[array, cut] = total.astype(jnp.bfloat16)
        core_copy(array, cut).start()
        home[array, my_group, :, cut_columns(cut)] = leaving_core[
            array, cut, pl.ds(my_group * visitors, visitors)
        ]

    def put_home(array, cut, result):
        core_wait(array, cut)
        found = home[array, :, :, cut_columns(cut)].reshape(block_rows, half_features)
        result[:, cut_columns(cut)] = lax.dot_general(
            place_table[...], found, (((0,), (0,)), ((), ())),
            preferred_element_type=jnp.float32,
        ).astype(jnp.bfloat16)

    for array in range(2):
        pair_copy(array).start()

    events = dict(
        gather=gather, separate=separate, multiply_in=multiply_in, multiply_grad=multiply_grad,
        activate_out=activate_out, activate_back=activate_back, multiply_out=multiply_out,
        multiply_back=multiply_back, give_back=give_back, finish=finish,
    )
    for name, *where in SCHEDULE:
        events[name](*where)

    for array, result in enumerate((layer_out, grad_in)):
        for cut in range(HALVES):
            put_home(array, cut, result)
    for array in range(2):
        pair_copy(array).wait_send()
        for step in range(lines):
            for index in range(groups):
                forward(sent, array, step, piece_at(index))
        for cut in range(HALVES):
            core_copy(array, cut).wait_send()
            for step in range(lines):
                side_copy(array, step, cut).wait_send()
            for step in range(1, lines):
                land_copy(array, step, cut).wait_send()
    for stage_index in range(HALVES):
        for kind in range(2):
            pre_copy(stage_index, kind).wait_send()
        grad_copy(stage_index).wait_send()


def dense_device(tokens, grad_out, expert_ids, gate_score, w_gate_up, w_down):
    groups = lax.axis_size("group")
    members = lax.axis_size("expert")
    per_column, features = tokens.shape
    hidden_size = w_gate_up.shape[3]
    lane_blocks = hidden_size // 128
    gate_rows = jnp.transpose(
        w_gate_up[0].reshape(features, 2, lane_blocks, 128), (0, 2, 1, 3)
    ).reshape(features * lane_blocks * 2, 128)
    down_weights = w_down[0]
    visitors = per_column // groups
    lines = members // LANES
    half_rows = members * per_column // HALVES
    half, full = jnp.bfloat16, jnp.float32
    passes = features // (2 * STRIP)
    chunks = 5 if passes % 5 == 0 else 1
    dma = pltpu.SemaphoreType.DMA
    piece = (groups, visitors, features)
    block = (per_column, features // HALVES)
    vmem = pl.BlockSpec(memory_space=pltpu.VMEM)
    anywhere = pl.BlockSpec(memory_space=pl.ANY)
    result = jax.ShapeDtypeStruct(tokens.shape, tokens.dtype)
    return pl.pallas_call(
        layer_kernel,
        out_shape=(result, result),
        in_specs=[vmem, vmem, vmem, vmem, anywhere, anywhere],
        out_specs=(vmem, vmem),
        scratch_shapes=[
            pltpu.VMEM(gate_rows.shape, half),
            pltpu.VMEM((features, 2 * hidden_size), half),
            pltpu.VMEM(down_weights.shape, half),
            pltpu.VMEM((2, *piece), half),
            pltpu.VMEM((2, members, *piece), half),
            pltpu.VMEM((HALVES, half_rows, 2 * hidden_size), full),
            pltpu.VMEM((HALVES, half_rows, hidden_size), full),
            pltpu.VMEM((HALVES, half_rows, 2 * hidden_size), half),
            pltpu.VMEM((HALVES, half_rows, hidden_size), half),
            pltpu.VMEM((HALVES, half_rows, 2 * hidden_size), half),
            pltpu.VMEM((HALVES, half_rows, hidden_size), half),
            pltpu.VMEM((half_rows, hidden_size), half),
            pltpu.VMEM((half_rows, 2 * hidden_size), half),
            pltpu.VMEM((2, HALVES, members, *block), half),
            pltpu.VMEM((2, HALVES, lines, *block), half),
            pltpu.VMEM((2, HALVES, lines, *block), half),
            pltpu.VMEM((2, HALVES, lines - 1, *block), half),
            pltpu.VMEM((2, HALVES, *block), half),
            pltpu.VMEM((2, *piece), half),
            pltpu.VMEM((members * per_column, 1), full),
            pltpu.VMEM((per_column, per_column), half),
            dma((chunks,)), dma(()), dma((2,)), dma((2,)),
            dma((3, 2, members, groups)), dma((2, members, groups)),
            dma((HALVES, 2)), dma((HALVES, 2)), dma((HALVES,)), dma((HALVES,)),
            dma((2, HALVES, lines)), dma((2, HALVES, lines)),
            dma((2, HALVES, lines - 1)), dma((2, HALVES, lines)),
            dma((2, HALVES)), dma((2, HALVES)),
        ],
        compiler_params=pltpu.CompilerParams(
            collective_id=0, has_side_effects=True, vmem_limit_bytes=58 << 20
        ),
        name="layer",
    )(
        tokens, grad_out, jnp.transpose(expert_ids), jnp.transpose(gate_score),
        gate_rows, down_weights,
    )


def on_device(tokens, grad_out, expert_ids, gate_score, w_gate_up, w_down):
    groups = lax.axis_size("group")
    members = lax.axis_size("expert")
    my_group = lax.axis_index("group")
    my_index = lax.axis_index("expert")
    per_column = tokens.shape[0]
    features = tokens.shape[1]
    visitors = per_column // 2
    top_count = expert_ids.shape[1]
    arrivals = groups * visitors
    capacity = min(arrivals, (3 * per_column * top_count + 2 * members - 1) // (2 * members))
    expert_rows = members * capacity
    weights = route_weights(gate_score).reshape(groups, members, per_column, top_count)
    pick_ids = expert_ids.reshape(groups, members, per_column, top_count)
    group_range = jnp.arange(groups, dtype=jnp.int32)
    my_picks = pick_ids[my_group, my_index]
    visits_mine = jnp.any(my_picks[:, :, None] // members == group_range, axis=1)
    leave_table = slot_matrix(visits_mine, visitors).astype(jnp.bfloat16)
    visits_here = jnp.any(pick_ids // members == my_group, axis=3)
    arrival_table = slot_matrix(visits_here[..., None], visitors)[:, :, 0]
    row_ids = jnp.einsum(
        "gest,getk->gesk", arrival_table, pick_ids.astype(jnp.float32), precision=HIGHEST
    )
    row_weights = jnp.einsum("gest,getk->gesk", arrival_table, weights, precision=HIGHEST)
    targets = (my_group * members + jnp.arange(members, dtype=jnp.int32)).astype(jnp.float32)
    matched = row_ids[..., None] == targets
    picked = jnp.any(matched, axis=3)
    picked_weight = jnp.sum(jnp.where(matched, row_weights[..., None], 0.0), axis=3)
    send_flags = picked[:, my_index].reshape(arrivals, members)
    send_table = slot_matrix(send_flags, capacity)
    send_share = jnp.transpose(picked_weight[:, my_index].reshape(arrivals, members))
    send_weight = send_table * send_share[:, None, :]
    came_flags = jnp.transpose(picked[:, :, :, my_index], (1, 0, 2)).reshape(members, arrivals)
    came_table = slot_matrix(came_flags[..., None], capacity)[:, 0]
    came_share = jnp.transpose(picked_weight[:, :, :, my_index], (1, 0, 2)).reshape(
        members, arrivals
    )
    slot_weight = jnp.einsum("ecr,er->ec", came_table, came_share, precision=HIGHEST).reshape(
        expert_rows
    )

    def dispatch(values):
        leaving = jnp.einsum(
            "gst,tf->gsf", leave_table, values, preferred_element_type=jnp.float32
        ).astype(jnp.bfloat16)
        arrived = across(leaving).reshape(arrivals, features)
        onward = jnp.einsum(
            "ecr,rf->ecf",
            send_table.astype(jnp.bfloat16),
            arrived,
            preferred_element_type=jnp.float32,
        ).astype(jnp.bfloat16)
        return within(onward).reshape(expert_rows, features)

    def combine(values, table):
        returned = within(values.reshape(members, capacity, features)).astype(jnp.float32)
        summed = jnp.einsum("ecr,ecf->rf", table, returned, precision=HIGHEST).astype(jnp.bfloat16)
        home = across(summed.reshape(groups, visitors, features))
        return jnp.einsum(
            "gst,gsf->tf", leave_table, home, preferred_element_type=jnp.float32
        ).astype(jnp.bfloat16)

    rows_in = dispatch(tokens)
    rows_grad = dispatch(grad_out)
    gate_weights = w_gate_up[0]
    down_weights = w_down[0]
    partial_value = jnp.einsum(
        "rf,fkh->rkh", rows_in, gate_weights, preferred_element_type=jnp.float32
    )
    grad_partial = jnp.einsum(
        "rf,hf->rh", rows_grad, down_weights, preferred_element_type=jnp.float32
    )
    empty_rows = jnp.zeros((expert_rows, features), jnp.float32)
    gate_both = share_sum(partial_value)
    gate_pre = gate_both[:, 0]
    up_pre = gate_both[:, 1]
    hidden = (jax.nn.silu(gate_pre) * up_pre).astype(jnp.bfloat16)[:, None, :]

    def down_step(running_sum, gathered, first_row):
        return jnp.dot(gathered[:, 0], down_weights, preferred_element_type=jnp.float32)

    expert_out = share_fold(hidden, down_step, empty_rows).astype(jnp.bfloat16)
    hidden_grad = share_sum(grad_partial[:, None, :])[:, 0] * slot_weight[:, None]
    pre_grad = local_grad(gate_pre, up_pre, hidden_grad)

    def input_step(running_sum, gathered, first_row):
        return jnp.einsum("rkh,fkh->rf", gathered, gate_weights, preferred_element_type=jnp.float32)

    expert_grad = share_fold(pre_grad, input_step, empty_rows).astype(jnp.bfloat16)
    layer_out = combine(expert_out, send_weight)
    grad_in = combine(expert_grad, send_table)
    return (layer_out, grad_in)


def per_device(tokens, grad_out, expert_ids, gate_score, w_gate_up, w_down):
    members = lax.axis_size("expert")
    dense = (
        expert_ids.shape[1] == members
        and members == LINES * LANES
        and lax.axis_size("group") == 2
        and lax.axis_size("dp") == 2
        and tokens.shape[0] == 2 * STRIP
        and tokens.shape[1] % (2 * TILE) == 0
        and w_gate_up.shape[3] % TILE == 0
    )
    plan = dense_device if dense else on_device
    return plan(tokens, grad_out, expert_ids, gate_score, w_gate_up, w_down)


def solution(mesh):
    return jax.shard_map(
        per_device,
        mesh=mesh,
        in_specs=(
            P(("group", "expert"), "dp"),
            P(("group", "expert"), "dp"),
            P(),
            P(),
            P(("group", "expert"), "dp", None, None),
            P(("group", "expert"), None, "dp"),
        ),
        out_specs=(P(("group", "expert"), "dp"), P(("group", "expert"), "dp")),
        check_vma=False,
    )
```

time: 107 us -> 82.1 us (0.77); the launches traced: 106 us -> 81.9 us
  matrix products: 20.7 us -> 0 us
  other arithmetic: 4.15 us -> 0 us
  local copies, waits for them, and re-layouts: 1.17 us -> 3.18 us
  starting transfers between devices: 1.47 us -> 0 us
    dot_general x8 -> x0, matrix products: 20.7 us -> none  [the longest x1 8.43 us: dense_device(): jnp.einsum('rf,fkh->rkh', rows_in, gate_weights, preferred_element_type=j...]
    unnamed x18 -> x2, local copies, waits for them, and re-layouts: 0.06 us -> 3.18 us
    another operation x3 -> x0, other arithmetic: 2.13 us -> none  [the longest x1 1.71 us: local_grad(): return jnp.stack([gate_grad, up_grad], axis=1).astype(jnp.bfloat16)]
    add x1 -> x0, other arithmetic: 1.74 us -> none  [dp_sum(): total = total + moving.astype(jnp.float32)]
    ppermute x2 -> x0, starting transfers between devices: 1.47 us -> none  [dp_sum(): moving = lax.ppermute(moving, 'dp', swap)]
    pallas_call x4 -> x1, Pallas kernels: 77.2 us -> 78.1 us  [dense_device(): pl.pallas_call(layer_kernel, out_shape=(result, result), in_specs=[vmem,...]
  transfers between devices with their start and end apart: 2 -> 0, of which waited for: 0 -> 0; matrix products, arithmetic and copies ran while one was open for 10% -> 0% of each run, Pallas kernels for 37% -> 0%
where the time goes in v1:
time: 82.1 us; the launch traced here: 81.9 us
  Pallas kernels  78.1 us (95%)
  local copies, waits for them, and re-layouts  3.18 us (4%)
    pallas_call x1, Pallas kernels, dense_device(): pl.pallas_call(layer_kernel, out_shape=(result, result), in_specs=[vmem,...  78.1 us
    unnamed x2, local copies, waits for them, and re-layouts  3.18 us

profile of v1, /device:TPU:1, one launch (start us, length us, event | category | flops | bytes accessed | tf_op | source)
XLA Modules:
  0.0 81.9 jit_solution(2535657447765522327)
XLA Ops:
  0.6 78.1 %layer.1 = (bf16[32,2560]{1,0:T(8,128)(2,1)}, bf16[32,2560]{1,0:T(8,128)(2,1)}) custom-call(bf16[32,2560]{1,0:T(8,128)(2,1)} %tokens.1, bf16[32,2560]{1,0:T(8,128)(2,1)} %grad_out.1, s32[8,512]{1,0:T(8,128)} %bitcast.10, f32[8,512]{1,0:T(8,128)} %bitcast.11, bf16[40960,128]{1,0:T(8,128)(2,1)} %bitcast.8, bf16[1024,2560]{1,0:T(8,128)(2,1)} %bitcast.9), custom_call_target="tpu_custom_call" | custom-call | tf_op jit(solution)/shard_map/layer/pallas_call | solution.py:579
  78.7 1.6 %copy.11 = bf16[32,2560]{1,0:T(8,128)(2,1)} copy(bf16[32,2560]{1,0:T(8,128)(2,1)} %get-tuple-element.4) | data formatting | bytes 327680
  80.3 1.6 %copy.12 = bf16[32,2560]{1,0:T(8,128)(2,1)} copy(bf16[32,2560]{1,0:T(8,128)(2,1)} %get-tuple-element.5) | data formatting | bytes 327680

commit v2 on v1

--- a/solution.py
+++ b/solution.py
@@ -59,61 +59,77 @@
 STRIP = 16
 HALVES = 2
 LINES = 4
+SPAN = 128
+BOTH_LANES = ((False, False), (False, True))
 SCHEDULE = (
     ("gather", 0, 0, 0),
     ("separate", 0),
+    ("separate", 1),
     ("gather", 0, 0, 1),
+    ("separate", 2),
     ("gather", 1, 0, 1),
-    ("separate", 1),
+    ("separate", 3),
     ("gather", 0, 1, 0),
-    ("separate", 2),
-    ("separate", 3),
+    ("separate", 4),
+    ("multiply_level", 0, 0),
     ("gather", 0, 1, 1),
     ("gather", 0, 2, 1),
+    ("multiply_level", 0, 1),
+    ("gather", 0, 2, 0),
+    ("gather", 1, 1, 1),
+    ("gather", 0, 3, 0),
+    ("multiply_level", 1, 0),
+    ("gather", 0, 3, 1),
     ("gather", 1, 0, 0),
-    ("separate", 4),
-    ("gather", 1, 1, 1),
-    ("multiply_in", 0, 0),
-    ("gather", 0, 2, 0),
-    ("multiply_in", 0, 1),
-    ("gather", 0, 3, 0),
-    ("gather", 0, 3, 1),
+    ("multiply_level", 1, 1),
+    ("gather", 1, 2, 0),
+    ("gather_beside", 1, 0, 1),
     ("gather", 1, 1, 0),
-    ("gather", 1, 2, 0),
+    ("multiply_in", 1, 0),
+    ("gather", 1, 2, 1),
+    ("activate_out", 0),
+    ("gather", 1, 3, 0),
+    ("gather_beside", 1, 1, 1),
+    ("multiply_in", 1, 1),
     ("gather", 1, 3, 1),
-    ("multiply_in", 1, 0),
-    ("gather", 1, 3, 0),
-    ("activate_out", 0),
     ("multiply_out", 0, 0),
-    ("multiply_in", 1, 1),
     ("multiply_out", 0, 1),
-    ("multiply_grad", 0),
-    ("gather", 1, 2, 1),
-    ("give_back", 0, 1, 1),
-    ("give_back", 0, 1, 0),
+    ("gather_beside", 1, 2, 1),
+    ("gather_beside", 1, 3, 1),
+    ("multiply_grad", 1),
     ("activate_out", 1),
     ("multiply_out", 1, 0),
-    ("multiply_grad", 1),
+    ("give_back", 0, 1, 0),
+    ("give_back", 0, 1, 1),
+    ("multiply_grad", 0),
     ("multiply_out", 1, 1),
     ("give_back", 0, 3, 0),
+    ("activate_back", 1),
+    ("give_back", 0, 2, 0),
+    ("multiply_back", 1, 0),
+    ("give_back", 0, 3, 1),
+    ("relay", 0, 3, 0),
+    ("multiply_back", 1, 1),
+    ("relay", 0, 2, 0),
+    ("give_back", 0, 2, 1),
+    ("give_back", 1, 3, 0),
     ("activate_back", 0),
-    ("give_back", 0, 2, 0),
+    ("relay", 0, 3, 1),
     ("multiply_back", 0, 0),
-    ("give_back", 0, 3, 1),
+    ("relay", 0, 2, 1),
+    ("give_back", 1, 3, 1),
+    ("relay", 1, 3, 0),
+    ("give_back", 1, 2, 0),
     ("multiply_back", 0, 1),
-    ("give_back", 0, 2, 1),
-    ("activate_back", 1),
+    ("give_back", 1, 2, 1),
     ("give_back", 1, 1, 0),
-    ("multiply_back", 1, 0),
+    ("relay", 1, 3, 1),
+    ("relay", 1, 2, 0),
+    ("give_back", 1, 1, 1),
+    ("relay", 1, 2, 1),
     ("finish", 0, 0),
-    ("give_back", 1, 1, 1),
-    ("multiply_back", 1, 1),
-    ("give_back", 1, 3, 0),
-    ("give_back", 1, 2, 0),
-    ("give_back", 1, 3, 1),
-    ("give_back", 1, 2, 1),
+    ("finish", 1, 0),
     ("finish", 0, 1),
-    ("finish", 1, 0),
     ("finish", 1, 1),
 )
 
@@ -129,12 +145,12 @@
 
 def layer_kernel(
     tokens, grad_out, ids, scores, gate_hbm, down_hbm,
-    layer_out, grad_in,
+    result,
     stage, weights, down, leaving, rows, own_pre, own_grad, out_pre, out_grad, in_pre, in_grad,
-    hidden, pre, parts, side, land, passing, leaving_core, home, share, place_table,
+    hidden, pre, parts, side, land, relayed, passing, leaving_core, home, share, place_table,
     stage_sem, down_sem, pair_send, pair_recv, row_send, row_recv,
-    pre_send, pre_recv, grad_send, grad_recv,
-    side_send, side_recv, land_send, land_recv, core_send, core_recv,
+    level_send, level_recv, pre_send, pre_recv, grad_send, grad_recv,
+    side_send, side_recv, land_send, land_recv, relay_recv, core_send, core_recv,
 ):
     my_group = lax.axis_index("group")
     me = lax.axis_index("expert")
@@ -153,6 +169,7 @@
     half_members = half_lines * LANES
     block_rows = groups * visitors
     half_rows = half_members * block_rows
+    level_rows = LANES * block_rows
     half_features = features // HALVES
     my_half = line // half_lines
     orders = visit_order(lines)
@@ -202,20 +219,28 @@
         )
 
     grouped = wide((ids[0:1, :] >= members).astype(jnp.int32))
-
-    def token_iota(dimension):
-        return lax.broadcasted_iota(jnp.int32, (token_count, token_count), dimension)
-
-    before, after = token_iota(0), token_iota(1)
+    spans = token_count // SPAN
+    folded = jnp.concatenate(
+        [grouped[:, part * SPAN:(part + 1) * SPAN] for part in range(spans)], axis=0
+    )
+
+    def span_iota(shape, dimension):
+        return lax.broadcasted_iota(jnp.int32, shape, dimension)
+
+    before, after = span_iota((SPAN, SPAN), 0), span_iota((SPAN, SPAN), 1)
     together = jnp.logical_and(before // per_column == after // per_column, before < after)
     ranked = half_dot(
-        jnp.concatenate([1.0 - grouped, grouped], axis=0), wide(together.astype(jnp.int32))
-    )
-    slot = jnp.where(grouped > 0.5, visitors + ranked[1:2], ranked[0:1])
+        jnp.concatenate([1.0 - folded, folded], axis=0), wide(together.astype(jnp.int32))
+    )
+    rank = jnp.where(folded > 0.5, ranked[spans:], ranked[:spans])
     first_token = (my_group * members + me) * per_column
-    token_of = lax.broadcasted_iota(jnp.int32, (token_count, per_column), 0)
-    column_of = lax.broadcasted_iota(jnp.int32, (token_count, per_column), 1)
-    own_slot = half_dot(slot, wide((token_of == first_token + column_of).astype(jnp.int32)))
+    span_row = span_iota((spans, SPAN), 0)
+    slots = jnp.where(span_row == first_token // SPAN, visitors * folded + rank, 0.0)
+    slot = jnp.sum(slots, axis=0, keepdims=True)
+    token_of = span_iota((SPAN, per_column), 0)
+    column_of = span_iota((SPAN, per_column), 1)
+    found_token = token_of == lax.rem(first_token, SPAN) + column_of
+    own_slot = half_dot(slot, wide(found_token.astype(jnp.int32)))
     row_of = lax.broadcasted_iota(jnp.int32, (block_rows, per_column), 0)
     place_table[...] = wide((wide(row_of) == own_slot).astype(jnp.int32)).astype(jnp.bfloat16)
     for array, values in enumerate((tokens, grad_out)):
@@ -252,17 +277,28 @@
 
     has_up = line < lines - 1
     has_down = line > 0
-
-    def forward(act, array, step, piece):
+    outer = jnp.logical_or(line == 0, line == lines - 1)
+
+    def along(act, array, step, block, piece):
         level = level_at(step)
-        block = level * LANES + lane
         pl.when(jnp.logical_and(level <= line, has_up))(
             lambda: act(hop(1, array, block, piece, me + LANES))
         )
         pl.when(jnp.logical_and(level >= line, has_down))(
             lambda: act(hop(2, array, block, piece, me - LANES))
         )
-        act(hop_side(array, block, piece))
+
+    def forward(act, array, step, index):
+        piece = piece_at(index)
+        block = level_at(step) * LANES + lane
+        if step == 0:
+            act(hop_side(array, block, piece))
+        along(act, array, step, block, piece)
+        if step and not BOTH_LANES[array][index]:
+            act(hop_side(array, block, piece))
+
+    def forward_beside(act, array, step, index):
+        along(act, array, step, level_at(step) * LANES + other_lane, piece_at(index))
 
     def piece_at(index):
         return my_group if index == 0 else other
@@ -281,13 +317,22 @@
                 pair_wait(array)
         else:
             hop_side(array, mine, piece).wait_recv()
-        forward(begin, array, step, piece)
+        forward(begin, array, step, index)
+
+    def gather_beside(array, step, index):
+        theirs = level_at(step) * LANES + other_lane
+        hop_side(array, theirs, piece_at(index)).wait_recv()
+        forward_beside(begin, array, step, index)
+
+    def gathered_level(array, step):
+        theirs = level_at(step) * LANES + other_lane
+        for index in range(groups):
+            if not BOTH_LANES[array][index]:
+                hop_side(array, theirs, piece_at(index)).wait_recv()
 
     def gathered(array, stage_index):
         for step in range(stage_index * half_lines, (stage_index + 1) * half_lines):
-            theirs = level_at(step) * LANES + other_lane
-            for index in range(groups):
-                hop_side(array, theirs, piece_at(index)).wait_recv()
+            gathered_level(array, step)
 
     span_rows = STRIP * 2 * (hidden_size // 128)
 
@@ -333,7 +378,7 @@
         columns = pl.ds(kind * hidden_size, hidden_size)
         return remote(
             out_pre.at[stage_index, :, columns], in_pre.at[stage_index, :, columns],
-            pre_send.at[stage_index, kind], pre_recv.at[stage_index, kind],
+            pre_send.at[kind], pre_recv.at[kind],
             {"dp": 1 - my_share},
         )
 
@@ -342,6 +387,27 @@
             out_grad.at[stage_index], in_grad.at[stage_index],
             grad_send.at[stage_index], grad_recv.at[stage_index], {"dp": 1 - my_share},
         )
+
+    def level_rows_of(step):
+        first = lax.rem(level_at(step), half_lines) * level_rows
+        return pl.ds(pl.multiple_of(first, level_rows), level_rows)
+
+    def level_copy(step, kind):
+        where = (0, level_rows_of(step), pl.ds(kind * hidden_size, hidden_size))
+        return remote(
+            out_pre.at[where], in_pre.at[where], level_send.at[step, kind],
+            level_recv.at[step, kind], {"dp": 1 - my_share},
+        )
+
+    def multiply_level(step, kind):
+        if kind == 0:
+            gathered_level(0, step)
+        columns = pl.ds(kind * hidden_size, hidden_size)
+        found = rows[0, pl.ds(level_at(step) * LANES, LANES)].reshape(level_rows, features)
+        value = jnp.dot(found, weights[:, columns], preferred_element_type=jnp.float32)
+        own_pre[0, level_rows_of(step), columns] = value
+        out_pre[0, level_rows_of(step), columns] = value.astype(jnp.bfloat16)
+        level_copy(step, kind).start()
 
     def multiply_in(stage_index, kind):
         if kind == 0:
@@ -355,8 +421,8 @@
         out_pre[stage_index, :, columns] = value.astype(jnp.bfloat16)
         pre_copy(stage_index, kind).start()
 
-    def down_ready(stage_index):
-        if stage_index == 0 and not waited:
+    def down_ready():
+        if not waited:
             waited.append(True)
             down_copy.wait()
 
@@ -364,7 +430,7 @@
 
     def multiply_grad(stage_index):
         gathered(1, stage_index)
-        down_ready(stage_index)
+        down_ready()
         value = lax.dot_general(
             half_block(1, half_at(stage_index)), down[...], (((1,), (1,)), ((), ())),
             preferred_element_type=jnp.float32,
@@ -381,8 +447,8 @@
         token = lax.broadcasted_iota(jnp.int32, (1, token_count), 1)
         member = lax.rem(token // per_column, members)
         source = token // (per_column * members)
-        rank = jnp.where(grouped > 0.5, ranked[1:2], ranked[0:1])
-        row = wide(member * block_rows + source * visitors) + rank
+        token_rank = jnp.concatenate([rank[part:part + 1] for part in range(spans)], axis=1)
+        row = wide(member * block_rows + source * visitors) + token_rank
         here = grouped == wide(my_group + jnp.zeros((1, token_count), jnp.int32))
         row = jnp.where(here, row, -1.0)
         at = wide(lax.broadcasted_iota(jnp.int32, (HALVES * half_rows, token_count), 0))
@@ -404,7 +470,11 @@
         if stage_index == 0:
             make_share()
         for kind in range(2):
-            pre_copy(stage_index, kind).wait_recv()
+            if stage_index:
+                pre_copy(stage_index, kind).wait_recv()
+                continue
+            for step in range(half_lines):
+                level_copy(step, kind).wait_recv()
         weight = half_share(stage_index)
 
         def one(index, carry):
@@ -426,7 +496,7 @@
         lax.fori_loop(0, hidden_size // TILE, one, 0)
 
     def multiply_out(stage_index, cut):
-        down_ready(stage_index)
+        down_ready()
         value = jnp.dot(
             hidden[...], down[:, cut * half_features:(cut + 1) * half_features],
             preferred_element_type=jnp.float32,
@@ -463,20 +533,23 @@
             {"expert": beside},
         )
 
-    def land_copy(array, step, cut):
+    def send_sum(array, step, cut, dst, recv, target):
         return remote(
-            passing.at[array, cut, step - 1], land.at[array, cut, line],
-            land_send.at[array, cut, step - 1], land_recv.at[array, cut, line],
-            {"expert": level_at(step) * LANES + lane},
-        )
-
-    def land_wait(array, step, cut):
-        source = level_at(step)
-        remote(
-            passing.at[array, cut, step - 1], land.at[array, cut, source],
-            land_send.at[array, cut, step - 1], land_recv.at[array, cut, source],
-            {"expert": source * LANES + lane},
-        ).wait_recv()
+            passing.at[array, cut, step - 1], dst, land_send.at[array, cut, step - 1], recv,
+            {"expert": target * LANES + lane},
+        )
+
+    def land_copy(array, step, cut, place):
+        return send_sum(
+            array, step, cut, land.at[array, cut, place], land_recv.at[array, cut, place],
+            level_at(step),
+        )
+
+    def relay_copy(array, step, cut):
+        return send_sum(
+            array, step, cut, relayed.at[array, cut, step - half_lines],
+            relay_recv.at[array, cut, step - half_lines], level_at(1),
+        )
 
     def pair_sum(array, step, cut):
         side_copy(array, step, cut).wait_recv()
@@ -484,8 +557,23 @@
         return wide(parts[array, cut, level * LANES + lane]) + wide(side[array, cut, level])
 
     def give_back(array, step, cut):
-        passing[array, cut, step - 1] = pair_sum(array, step, cut).astype(jnp.bfloat16)
-        land_copy(array, step, cut).start()
+        def send(copy):
+            passing[array, cut, step - 1] = pair_sum(array, step, cut).astype(jnp.bfloat16)
+            copy.start()
+
+        if step < half_lines:
+            send(land_copy(array, step, cut, 0))
+        else:
+            pl.when(outer)(lambda: send(relay_copy(array, step, cut)))
+
+    def relay(array, step, cut):
+        @pl.when(jnp.logical_not(outer))
+        def _():
+            value = pair_sum(array, step, cut)
+            relay_copy(array, step, cut).wait_recv()
+            value = value + wide(relayed[array, cut, step - half_lines])
+            passing[array, cut, step - 1] = value.astype(jnp.bfloat16)
+            land_copy(array, step, cut, 1).start()
 
     def cut_columns(cut):
         return pl.ds(cut * half_features, half_features)
@@ -506,19 +594,19 @@
 
     def finish(array, cut):
         total = pair_sum(array, 0, cut)
-        for step in range(1, lines):
-            land_wait(array, step, cut)
-            total = total + wide(land[array, cut, level_at(step)])
+        for place in range(HALVES):
+            land_copy(array, 1, cut, place).wait_recv()
+            total = total + wide(land[array, cut, place])
         leaving_core[array, cut] = total.astype(jnp.bfloat16)
         core_copy(array, cut).start()
         home[array, my_group, :, cut_columns(cut)] = leaving_core[
             array, cut, pl.ds(my_group * visitors, visitors)
         ]
 
-    def put_home(array, cut, result):
+    def put_home(array, cut):
         core_wait(array, cut)
         found = home[array, :, :, cut_columns(cut)].reshape(block_rows, half_features)
-        result[:, cut_columns(cut)] = lax.dot_general(
+        result[array, :, cut_columns(cut)] = lax.dot_general(
             place_table[...], found, (((0,), (0,)), ((), ())),
             preferred_element_type=jnp.float32,
         ).astype(jnp.bfloat16)
@@ -528,29 +616,33 @@
 
     events = dict(
         gather=gather, separate=separate, multiply_in=multiply_in, multiply_grad=multiply_grad,
-        activate_out=activate_out, activate_back=activate_back, multiply_out=multiply_out,
+        activate_out=activate_out, gather_beside=gather_beside, multiply_level=multiply_level, relay=relay, activate_back=activate_back, multiply_out=multiply_out,
         multiply_back=multiply_back, give_back=give_back, finish=finish,
     )
     for name, *where in SCHEDULE:
         events[name](*where)
 
-    for array, result in enumerate((layer_out, grad_in)):
+    for array in range(2):
         for cut in range(HALVES):
-            put_home(array, cut, result)
+            put_home(array, cut)
     for array in range(2):
         pair_copy(array).wait_send()
         for step in range(lines):
             for index in range(groups):
-                forward(sent, array, step, piece_at(index))
+                forward(sent, array, step, index)
+                if BOTH_LANES[array][index]:
+                    forward_beside(sent, array, step, index)
         for cut in range(HALVES):
             core_copy(array, cut).wait_send()
             for step in range(lines):
                 side_copy(array, step, cut).wait_send()
             for step in range(1, lines):
-                land_copy(array, step, cut).wait_send()
+                land_copy(array, step, cut, 0).wait_send()
+    for kind in range(2):
+        pre_copy(1, kind).wait_send()
+        for step in range(half_lines):
+            level_copy(step, kind).wait_send()
     for stage_index in range(HALVES):
-        for kind in range(2):
-            pre_copy(stage_index, kind).wait_send()
         grad_copy(stage_index).wait_send()
 
 
@@ -575,12 +667,11 @@
     block = (per_column, features // HALVES)
     vmem = pl.BlockSpec(memory_space=pltpu.VMEM)
     anywhere = pl.BlockSpec(memory_space=pl.ANY)
-    result = jax.ShapeDtypeStruct(tokens.shape, tokens.dtype)
-    return pl.pallas_call(
+    found = pl.pallas_call(
         layer_kernel,
-        out_shape=(result, result),
+        out_shape=jax.ShapeDtypeStruct((2, *tokens.shape), half),
         in_specs=[vmem, vmem, vmem, vmem, anywhere, anywhere],
-        out_specs=(vmem, vmem),
+        out_specs=vmem,
         scratch_shapes=[
             pltpu.VMEM(gate_rows.shape, half),
             pltpu.VMEM((features, 2 * hidden_size), half),
@@ -597,7 +688,8 @@
             pltpu.VMEM((half_rows, 2 * hidden_size), half),
             pltpu.VMEM((2, HALVES, members, *block), half),
             pltpu.VMEM((2, HALVES, lines, *block), half),
-            pltpu.VMEM((2, HALVES, lines, *block), half),
+            pltpu.VMEM((2, HALVES, HALVES, *block), half),
+            pltpu.VMEM((2, HALVES, lines // HALVES, *block), half),
             pltpu.VMEM((2, HALVES, lines - 1, *block), half),
             pltpu.VMEM((2, HALVES, *block), half),
             pltpu.VMEM((2, *piece), half),
@@ -605,9 +697,11 @@
             pltpu.VMEM((per_column, per_column), half),
             dma((chunks,)), dma(()), dma((2,)), dma((2,)),
             dma((3, 2, members, groups)), dma((2, members, groups)),
-            dma((HALVES, 2)), dma((HALVES, 2)), dma((HALVES,)), dma((HALVES,)),
+            dma((lines // HALVES, 2)), dma((lines // HALVES, 2)),
+            dma((2,)), dma((2,)), dma((HALVES,)), dma((HALVES,)),
             dma((2, HALVES, lines)), dma((2, HALVES, lines)),
-            dma((2, HALVES, lines - 1)), dma((2, HALVES, lines)),
+            dma((2, HALVES, lines - 1)), dma((2, HALVES, HALVES)),
+            dma((2, HALVES, lines // HALVES)),
             dma((2, HALVES)), dma((2, HALVES)),
         ],
         compiler_params=pltpu.CompilerParams(
@@ -618,6 +712,7 @@
         tokens, grad_out, jnp.transpose(expert_ids), jnp.transpose(gate_score),
         gate_rows, down_weights,
     )
+    return found[0], found[1]
 
 
 def on_device(tokens, grad_out, expert_ids, gate_score, w_gate_up, w_down):
@@ -722,6 +817,7 @@
         and lax.axis_size("group") == 2
         and lax.axis_size("dp") == 2
         and tokens.shape[0] == 2 * STRIP
+        and expert_ids.shape[0] % SPAN == 0
         and tokens.shape[1] % (2 * TILE) == 0
         and w_gate_up.shape[3] % TILE == 0
     )

time: 82.1 us -> 74.9 us (0.912)
  Pallas kernels: 78.1 us -> 72.3 us
  local copies, waits for them, and re-layouts: 3.18 us -> 1.74 us
    pallas_call x1, Pallas kernels: 78.1 us -> 72.3 us  [dense_device(): pl.pallas_call(layer_kernel, out_shape=jax.ShapeDtypeStruct((2, *tokens.s...]
    unnamed x2 -> x0, local copies, waits for them, and re-layouts: 3.18 us -> none
    squeeze x0 -> x1, local copies, waits for them, and re-layouts: none -> 1.74 us  [dense_device(): return (found[0], found[1])]
where the time goes in v2:
time: 74.9 us; the launch traced here: 74.7 us
  Pallas kernels  72.3 us (97%)
  local copies, waits for them, and re-layouts  1.74 us (2%)
    pallas_call x1, Pallas kernels, dense_device(): pl.pallas_call(layer_kernel, out_shape=jax.ShapeDtypeStruct((2, *tokens.s...  72.3 us
    squeeze x1, local copies, waits for them, and re-layouts, dense_device(): return (found[0], found[1])  1.74 us

profile of v2, /device:TPU:1, one launch (start us, length us, event | category | flops | bytes accessed | tf_op | source)
XLA Modules:
  0.0 74.7 jit_solution(9882591216791358846)
XLA Ops:
  0.6 72.3 %layer.1 = bf16[2,32,2560]{2,1,0:T(8,128)(2,1)} custom-call(bf16[32,2560]{1,0:T(8,128)(2,1)} %tokens.1, bf16[32,2560]{1,0:T(8,128)(2,1)} %grad_out.1, s32[8,512]{1,0:T(8,128)} %bitcast.14, f32[8,512]{1,0:T(8,128)} %bitcast.15, bf16[40960,128]{1,0:T(8,128)(2,1)} %bitcast.12, bf16[1024,2560]{1,0:T(8,128)(2,1)} %bitcast.13), custom_call_target="tpu_custom_call" | custom-call | tf_op jit(solution)/shard_map/layer/pallas_call | solution.py:670
  73.0 1.7 %slice_bitcast_fusion = (bf16[32,2560]{1,0:T(8,128)(2,1)}, bf16[32,2560]{1,0:T(8,128)(2,1)}) fusion(bf16[2,32,2560]{2,1,0:T(8,128)(2,1)} %layer.1), kind=kLoop, calls=%fused_computation | loop fusion | bytes 655360 | tf_op jit(solution)/shard_map/squeeze | solution.py:715

commit v3 on v2

--- a/solution.py
+++ b/solution.py
@@ -130,7 +130,11 @@
     ("finish", 0, 0),
     ("finish", 1, 0),
     ("finish", 0, 1),
+    ("put_home", 0, 0),
+    ("put_home", 0, 1),
+    ("put_home", 1, 0),
     ("finish", 1, 1),
+    ("put_home", 1, 1),
 )
 
 
@@ -144,11 +148,11 @@
 
 
 def layer_kernel(
-    tokens, grad_out, ids, scores, gate_hbm, down_hbm,
+    tokens_hbm, grad_hbm, ids_hbm, scores_hbm, gate_hbm, down_hbm,
     result,
-    stage, weights, down, leaving, rows, own_pre, own_grad, out_pre, out_grad, in_pre, in_grad,
+    tokens, grad_out, ids, scores, stage, weights, down, leaving, rows, own_pre, own_grad, out_pre, out_grad, in_pre, in_grad,
     hidden, pre, parts, side, land, relayed, passing, leaving_core, home, share, place_table,
-    stage_sem, down_sem, pair_send, pair_recv, row_send, row_recv,
+    input_sem, stage_sem, down_sem, pair_send, pair_recv, row_send, row_recv,
     level_send, level_recv, pre_send, pre_recv, grad_send, grad_recv,
     side_send, side_recv, land_send, land_recv, relay_recv, core_send, core_recv,
 ):
@@ -172,6 +176,9 @@
     level_rows = LANES * block_rows
     half_features = features // HALVES
     my_half = line // half_lines
+    has_up = line < lines - 1
+    has_down = line > 0
+    outer = jnp.logical_or(line == 0, line == lines - 1)
     orders = visit_order(lines)
     chunks = stage_sem.shape[0]
 
@@ -195,6 +202,13 @@
         )
     down_copy = pltpu.make_async_copy(down_hbm, down, down_sem)
 
+    inputs = ((ids_hbm, ids), (tokens_hbm, tokens), (grad_hbm, grad_out), (scores_hbm, scores))
+    input_copies = [
+        pltpu.make_async_copy(src, dst, input_sem.at[index])
+        for index, (src, dst) in enumerate(inputs)
+    ]
+    for copy in input_copies:
+        copy.start()
     barrier = pltpu.get_barrier_semaphore()
 
     def hello(where):
@@ -203,11 +217,16 @@
     hello({"group": other})
     hello({"expert": beside})
     hello({"dp": 1 - my_share})
-    for step in range(1, lines):
+    for step in range(1, lines - 1):
         hello({"expert": level_at(step) * LANES + lane})
+    pl.when(jnp.logical_not(outer))(
+        lambda: hello({"expert": level_at(lines - 1) * LANES + lane})
+    )
     for copy in stage_copies:
         copy.start()
     down_copy.start()
+    for copy in input_copies:
+        copy.wait()
 
     def wide(value):
         return value.astype(jnp.float32)
@@ -251,7 +270,7 @@
             leaving[array, group] = moved[group * visitors:(group + 1) * visitors]
         rows[array, me, my_group] = leaving[array, my_group]
 
-    pl.semaphore_wait(barrier, 3 + lines - 1)
+    pl.semaphore_wait(barrier, 3 + lines - 1 - outer.astype(jnp.int32))
 
     def pair_copy(array):
         return remote(
@@ -275,9 +294,6 @@
     def hop_side(array, block, piece):
         return hop(0, array, block, piece, beside)
 
-    has_up = line < lines - 1
-    has_down = line > 0
-    outer = jnp.logical_or(line == 0, line == lines - 1)
 
     def along(act, array, step, block, piece):
         level = level_at(step)
@@ -617,14 +633,11 @@
     events = dict(
         gather=gather, separate=separate, multiply_in=multiply_in, multiply_grad=multiply_grad,
         activate_out=activate_out, gather_beside=gather_beside, multiply_level=multiply_level, relay=relay, activate_back=activate_back, multiply_out=multiply_out,
-        multiply_back=multiply_back, give_back=give_back, finish=finish,
+        multiply_back=multiply_back, give_back=give_back, finish=finish, put_home=put_home,
     )
     for name, *where in SCHEDULE:
         events[name](*where)
 
-    for array in range(2):
-        for cut in range(HALVES):
-            put_home(array, cut)
     for array in range(2):
         pair_copy(array).wait_send()
         for step in range(lines):
@@ -666,13 +679,17 @@
     piece = (groups, visitors, features)
     block = (per_column, features // HALVES)
     vmem = pl.BlockSpec(memory_space=pltpu.VMEM)
-    anywhere = pl.BlockSpec(memory_space=pl.ANY)
+    in_hbm = pl.BlockSpec(memory_space=pltpu.HBM)
     found = pl.pallas_call(
         layer_kernel,
         out_shape=jax.ShapeDtypeStruct((2, *tokens.shape), half),
-        in_specs=[vmem, vmem, vmem, vmem, anywhere, anywhere],
+        in_specs=[in_hbm] * 6,
         out_specs=vmem,
         scratch_shapes=[
+            pltpu.VMEM(tokens.shape, half),
+            pltpu.VMEM(tokens.shape, half),
+            pltpu.VMEM(expert_ids.shape[::-1], jnp.int32),
+            pltpu.VMEM(gate_score.shape[::-1], full),
             pltpu.VMEM(gate_rows.shape, half),
             pltpu.VMEM((features, 2 * hidden_size), half),
             pltpu.VMEM(down_weights.shape, half),
@@ -695,7 +712,7 @@
             pltpu.VMEM((2, *piece), half),
             pltpu.VMEM((members * per_column, 1), full),
             pltpu.VMEM((per_column, per_column), half),
-            dma((chunks,)), dma(()), dma((2,)), dma((2,)),
+            dma((4,)), dma((chunks,)), dma(()), dma((2,)), dma((2,)),
             dma((3, 2, members, groups)), dma((2, members, groups)),
             dma((lines // HALVES, 2)), dma((lines // HALVES, 2)),
             dma((2,)), dma((2,)), dma((HALVES,)), dma((HALVES,)),
@@ -705,13 +722,16 @@
             dma((2, HALVES)), dma((2, HALVES)),
         ],
         compiler_params=pltpu.CompilerParams(
-            collective_id=0, has_side_effects=True, vmem_limit_bytes=58 << 20
+            collective_id=0, has_side_effects=True, vmem_limit_bytes=48 << 20
         ),
         name="layer",
-    )(
-        tokens, grad_out, jnp.transpose(expert_ids), jnp.transpose(gate_score),
-        gate_rows, down_weights,
-    )
+    )(*[
+        pltpu.with_memory_space_constraint(value, pltpu.HBM)
+        for value in (
+            tokens, grad_out, jnp.transpose(expert_ids), jnp.transpose(gate_score),
+            gate_rows, down_weights,
+        )
+    ])
     return found[0], found[1]
 
 

time: 74.9 us -> 73.4 us (0.980)
  local copies, waits for them, and re-layouts: 1.74 us -> 0.74 us
    squeeze x1, local copies, waits for them, and re-layouts: 1.74 us -> 0.74 us  [dense_device(): return (found[0], found[1])]
where the time goes in v3:
time: 73.4 us; the launch traced here: 73.1 us
  Pallas kernels  71.7 us (98%)
  local copies, waits for them, and re-layouts  0.74 us (1%)
    pallas_call x1, Pallas kernels, dense_device(): pl.pallas_call(layer_kernel, out_shape=jax.ShapeDtypeStruct((2, *tokens.s...  71.7 us

profile of v3, /device:TPU:1, one launch (start us, length us, event | category | flops | bytes accessed | tf_op | source)
XLA Modules:
  0.0 73.1 jit_solution(7075575522210696358)
XLA Ops:
  0.6 71.7 %layer.1 = bf16[2,32,2560]{2,1,0:T(8,128)(2,1)S(1)} custom-call(bf16[32,2560]{1,0:T(8,128)(2,1)} %tokens_hbm.1, bf16[32,2560]{1,0:T(8,128)(2,1)} %grad_hbm.1, s32[8,512]{1,0:T(8,128)} %bitcast.14, f32[8,512]{1,0:T(8,128)} %bitcast.15, bf16[40960,128]{1,0:T(8,128)(2,1)} %bitcast.12, bf16[1024,2560]{1,0:T(8,128)(2,1)} %bitcast.13), custom_call_target="tpu_custom_call" | custom-call | tf_op jit(solution)/shard_map/layer/pallas_call | solution.py:683
  72.4 0.7 %slice_bitcast_fusion = (bf16[32,2560]{1,0:T(8,128)(2,1)}, bf16[32,2560]{1,0:T(8,128)(2,1)}) fusion(bf16[2,32,2560]{2,1,0:T(8,128)(2,1)S(1)} %layer.1), kind=kLoop, calls=%fused_computation | loop fusion | bytes 655360 | tf_op jit(solution)/shard_map/squeeze | solution.py:735

commit v4 on v3

--- a/solution.py
+++ b/solution.py
@@ -60,42 +60,42 @@
 HALVES = 2
 LINES = 4
 SPAN = 128
-BOTH_LANES = ((False, False), (False, True))
+BOTH_LANES = ((False, False), (True, False))
 SCHEDULE = (
     ("gather", 0, 0, 0),
     ("separate", 0),
+    ("gather", 0, 0, 1),
+    ("gather", 1, 0, 0),
     ("separate", 1),
-    ("gather", 0, 0, 1),
     ("separate", 2),
-    ("gather", 1, 0, 1),
+    ("gather", 0, 1, 0),
     ("separate", 3),
-    ("gather", 0, 1, 0),
     ("separate", 4),
+    ("gather", 0, 1, 1),
     ("multiply_level", 0, 0),
-    ("gather", 0, 1, 1),
+    ("gather", 0, 2, 0),
+    ("multiply_level", 0, 1),
     ("gather", 0, 2, 1),
-    ("multiply_level", 0, 1),
-    ("gather", 0, 2, 0),
-    ("gather", 1, 1, 1),
     ("gather", 0, 3, 0),
     ("multiply_level", 1, 0),
     ("gather", 0, 3, 1),
-    ("gather", 1, 0, 0),
+    ("gather", 1, 0, 1),
     ("multiply_level", 1, 1),
     ("gather", 1, 2, 0),
-    ("gather_beside", 1, 0, 1),
+    ("gather_beside", 1, 0, 0),
+    ("multiply_in", 1, 0),
+    ("gather", 1, 1, 1),
+    ("multiply_in", 1, 1),
     ("gather", 1, 1, 0),
-    ("multiply_in", 1, 0),
     ("gather", 1, 2, 1),
     ("activate_out", 0),
+    ("gather", 1, 3, 1),
+    ("gather_beside", 1, 1, 0),
+    ("multiply_out", 0, 0),
     ("gather", 1, 3, 0),
-    ("gather_beside", 1, 1, 1),
-    ("multiply_in", 1, 1),
-    ("gather", 1, 3, 1),
-    ("multiply_out", 0, 0),
     ("multiply_out", 0, 1),
-    ("gather_beside", 1, 2, 1),
-    ("gather_beside", 1, 3, 1),
+    ("gather_beside", 1, 2, 0),
+    ("gather_beside", 1, 3, 0),
     ("multiply_grad", 1),
     ("activate_out", 1),
     ("multiply_out", 1, 0),
@@ -108,28 +108,28 @@
     ("give_back", 0, 2, 0),
     ("multiply_back", 1, 0),
     ("give_back", 0, 3, 1),
+    ("give_back", 0, 2, 1),
+    ("multiply_back", 1, 1),
     ("relay", 0, 3, 0),
-    ("multiply_back", 1, 1),
+    ("activate_back", 0),
+    ("give_back", 1, 3, 0),
     ("relay", 0, 2, 0),
-    ("give_back", 0, 2, 1),
-    ("give_back", 1, 3, 0),
-    ("activate_back", 0),
+    ("give_back", 1, 2, 0),
+    ("multiply_back", 0, 0),
     ("relay", 0, 3, 1),
-    ("multiply_back", 0, 0),
     ("relay", 0, 2, 1),
     ("give_back", 1, 3, 1),
+    ("multiply_back", 0, 1),
     ("relay", 1, 3, 0),
-    ("give_back", 1, 2, 0),
-    ("multiply_back", 0, 1),
     ("give_back", 1, 2, 1),
     ("give_back", 1, 1, 0),
+    ("relay", 1, 2, 0),
     ("relay", 1, 3, 1),
-    ("relay", 1, 2, 0),
+    ("finish", 0, 0),
+    ("finish", 0, 1),
     ("give_back", 1, 1, 1),
     ("relay", 1, 2, 1),
-    ("finish", 0, 0),
     ("finish", 1, 0),
-    ("finish", 0, 1),
     ("put_home", 0, 0),
     ("put_home", 0, 1),
     ("put_home", 1, 0),

time: 73.4 us -> 69.3 us (0.944)
  Pallas kernels: 71.7 us -> 67.3 us
    pallas_call x1, Pallas kernels: 71.7 us -> 67.3 us  [dense_device(): pl.pallas_call(layer_kernel, out_shape=jax.ShapeDtypeStruct((2, *tokens.s...]
where the time goes in v4:
time: 69.3 us; the launch traced here: 68.7 us
  Pallas kernels  67.3 us (97%)
  local copies, waits for them, and re-layouts  0.74 us (1%)
    pallas_call x1, Pallas kernels, dense_device(): pl.pallas_call(layer_kernel, out_shape=jax.ShapeDtypeStruct((2, *tokens.s...  67.3 us

profile of v4, /device:TPU:1, one launch (start us, length us, event | category | flops | bytes accessed | tf_op | source)
XLA Modules:
  0.0 68.7 jit_solution(14899617813688505500)
XLA Ops:
  0.6 67.3 %layer.1 = bf16[2,32,2560]{2,1,0:T(8,128)(2,1)S(1)} custom-call(bf16[32,2560]{1,0:T(8,128)(2,1)} %tokens_hbm.1, bf16[32,2560]{1,0:T(8,128)(2,1)} %grad_hbm.1, s32[8,512]{1,0:T(8,128)} %bitcast.14, f32[8,512]{1,0:T(8,128)} %bitcast.15, bf16[40960,128]{1,0:T(8,128)(2,1)} %bitcast.12, bf16[1024,2560]{1,0:T(8,128)(2,1)} %bitcast.13), custom_call_target="tpu_custom_call" | custom-call | tf_op jit(solution)/shard_map/layer/pallas_call | solution.py:683
  67.9 0.7 %slice_bitcast_fusion = (bf16[32,2560]{1,0:T(8,128)(2,1)}, bf16[32,2560]{1,0:T(8,128)(2,1)}) fusion(bf16[2,32,2560]{2,1,0:T(8,128)(2,1)S(1)} %layer.1), kind=kLoop, calls=%fused_computation | loop fusion | bytes 655360 | tf_op jit(solution)/shard_map/squeeze | solution.py:735
